TPU v7x, 128 devices: a whole 4x4x4 slice. The times are simulated.
128 devices in a mesh: gx: 8 (over y, core), gy: 16 (over z, x).
Axes of the slice: x: 4, y: 4, z: 4, core: 2. Of those that a mesh axis runs over, the one named last changes fastest.
Arguments:
- source_mass: float32 [4, 2048, 2048], P(None, 'gx', 'gy'), may hold values from 0.1 to 2
- target_density: float32 [4, 2048, 2048], P(None, 'gx', 'gy'), may hold values from 0.25 to 4
- potential: float32 [4, 2048, 2048], P(None, 'gx', 'gy'), may hold values from -6 to 6
- dest_device: int32 [8, 16, 128, 4], P('gx', 'gy'), may hold values from 0 to 127, all different within a row; in each aligned block of 128 rows (0 to 127, 128 to 255, ..., all dimensions but the last counted through in order) at most 6 rows name the same one
- dest_tile: int32 [8, 16, 128, 4], P('gx', 'gy'), may hold values from 0 to 127
- mass_counts: int32 [8, 16, 128, 4], P('gx', 'gy'), may hold values from 1 to 8
- reach: float32 [4], replicated, may hold values from 2 to 16384
Outputs:
- pushed: float32 [4, 2048, 2048], P(None, 'gx', 'gy')
- potential_next: float32 [4, 2048, 2048], P(None, 'gx', 'gy')
Inputs may be any that keep to these rules, and one draw needn't show every extreme that they name: `dest_device`: within one block's 128 x 4 entries no destination block is named more than 6 times, and in some blocks one is named exactly 6 times; the 4 entries of one source tile name different blocks.
All inputs are finite; a program needn't handle non-finite values.
Results may differ from a plain program's by a relative error of at most 0.0001.
Values sent between devices are 32-bit elements; how exact they have to be, the bound alone decides.
A program may use at most 64 MiB of HBM per device.

v0:
```python
import jax
import jax.numpy as jnp
from jax import lax
from jax.sharding import PartitionSpec as P

TS = 16


def entering_2(array, axis, combine, identity, reverse):
    devices, position = (lax.axis_size(axis), lax.axis_index(axis))
    everything = jax.tree.map(lambda part: lax.all_gather(part, axis), array)
    start = jax.tree.map(
        lambda part, zero: jnp.broadcast_to(jnp.asarray(zero, part.dtype), part.shape),
        array,
        identity,
    )

    def step(k, before):
        at = devices - 1 - k if reverse else k
        reached = at > position if reverse else at < position
        new = combine(before, jax.tree.map(lambda part: part[at], everything))
        return jax.tree.map(lambda a, b: jnp.where(reached, a, b), new, before)

    return lax.fori_loop(0, devices, step, start)


def line_tables(reach, length):
    decay = 1.0 - 1.0 / reach
    logs = jnp.log(decay)[:, None, None]
    rows = lax.broadcasted_iota(jnp.float32, (1, length, length), 1)
    cols = lax.broadcasted_iota(jnp.float32, (1, length, length), 2)
    spacing = rows - cols
    lower = jnp.where(spacing >= 0.0, jnp.exp(jnp.maximum(spacing, 0.0) * logs), 0.0)
    place = lax.broadcasted_iota(jnp.float32, (1, length), 1)
    rise = jnp.exp((place + 1.0) * logs[:, :, 0])
    fall = jnp.exp((length - place) * logs[:, :, 0])
    across = jnp.exp(length * logs[:, :, 0])
    scale = ((1.0 - decay) ** 2)[:, None, None]
    return (lower, rise, fall, across, scale)


def compose(former, latter):
    return (former[0] * latter[0], latter[0] * former[1] + latter[1])


def ahead_x(lower, field):
    return jnp.einsum("zij,zjy->ziy", lower, field, precision=lax.Precision.HIGHEST)


def finish_x(local, tables):
    lower, rise, fall, across, scale = tables
    start = (jnp.ones_like(across), jnp.zeros_like(local[:, -1, :]))
    entering = entering_2((across, local[:, -1, :]), "gx", compose, start, False)[1]
    running = local + rise[:, :, None] * entering[:, None, :]
    base = scale * jnp.einsum("zji,zjy->ziy", lower, running, precision=lax.Precision.HIGHEST)
    leaving = entering_2((across, base[:, 0, :]), "gx", compose, start, True)[1]
    return base + fall[:, :, None] * leaving[:, None, :]


def sweep_y(field, tables):
    lower, rise, fall, across, scale = tables
    local = jnp.einsum("zij,zxj->zxi", lower, field, precision=lax.Precision.HIGHEST)
    start = (jnp.ones_like(across), jnp.zeros_like(local[:, :, -1]))
    entering = entering_2((across, local[:, :, -1]), "gy", compose, start, False)[1]
    running = local + rise[:, None, :] * entering[:, :, None]
    base = scale * jnp.einsum("zji,zxj->zxi", lower, running, precision=lax.Precision.HIGHEST)
    leaving = entering_2((across, base[:, :, 0]), "gy", compose, start, True)[1]
    return base + fall[:, None, :] * leaving[:, :, None]


def per_device(source_mass, target_density, potential, dest_device, dest_tile, mass_counts, reach):
    planes, cells_x, cells_y = source_mass.shape
    tile_count = dest_device.shape[2]
    fanout = dest_device.shape[3]
    tiles_x = cells_x // TS
    tiles_y = cells_y // TS
    tile_cells = planes * TS * TS
    grid_x = lax.axis_size("gx")
    grid_y = lax.axis_size("gy")
    device_count = grid_x * grid_y
    capacity = max(2, 3 * fanout * tile_count // (2 * device_count))
    entries = tile_count * fanout
    tables_x = line_tables(reach, cells_x)
    tables_y = line_tables(reach, cells_y)
    tiles = (
        source_mass.reshape(planes, tiles_x, TS, tiles_y, TS)
        .transpose(1, 3, 0, 2, 4)
        .reshape(tile_count, tile_cells)
    )
    counts = mass_counts.reshape(tile_count, fanout).astype(jnp.float32)
    shares = (counts / jnp.sum(counts, axis=1, keepdims=True)).reshape(entries)
    targets = dest_device.reshape(entries)
    target_tiles = dest_tile.reshape(entries)
    matches = (targets[:, None] == jnp.arange(device_count, dtype=jnp.int32)[None, :]).astype(
        jnp.int32
    )
    earlier_count = jnp.cumsum(matches, axis=0) - matches
    ranking = jnp.sum(earlier_count * matches, axis=1)
    slot_of = targets * capacity + ranking
    owner = (
        jnp.full((device_count * capacity,), entries, jnp.int32)
        .at[slot_of]
        .set(jnp.arange(entries, dtype=jnp.int32))
    )
    filled = owner < entries
    owner_safe = jnp.minimum(owner, entries - 1)
    weights = jnp.where(filled, shares[owner_safe], 0.0)
    outgoing = tiles[owner_safe // fanout] * weights[:, None]
    labels = jnp.where(filled, target_tiles[owner_safe], tile_count)
    arrived, arrived_labels = (
        lax.all_to_all(
            outgoing.reshape(device_count, capacity, tile_cells),
            ("gx", "gy"),
            split_axis=0,
            concat_axis=0,
            tiled=True,
        ),
        lax.all_to_all(
            labels.reshape(device_count, capacity),
            ("gx", "gy"),
            split_axis=0,
            concat_axis=0,
            tiled=True,
        ),
    )
    arrived = arrived.reshape(device_count * capacity, tile_cells)
    arrived_labels = arrived_labels.reshape(device_count * capacity)
    collect = (jnp.arange(tile_count, dtype=jnp.int32)[:, None] == arrived_labels[None, :]).astype(
        jnp.float32
    )
    pushed_tiles = jnp.dot(collect, arrived, precision=lax.Precision.HIGHEST)
    pushed = (
        pushed_tiles.reshape(tiles_x, tiles_y, planes, TS, TS)
        .transpose(2, 0, 3, 1, 4)
        .reshape(planes, cells_x, cells_y)
    )
    local = ahead_x(tables_x[0], target_density - pushed)
    smoothed_x = finish_x(local, tables_x)
    correction = sweep_y(smoothed_x, tables_y)
    return (pushed, potential + correction)


def solution(mesh):
    in_specs = (
        P(None, "gx", "gy"),
        P(None, "gx", "gy"),
        P(None, "gx", "gy"),
        P("gx", "gy", None, None),
        P("gx", "gy", None, None),
        P("gx", "gy", None, None),
        P(),
    )
    out_specs = (P(None, "gx", "gy"), P(None, "gx", "gy"))
    return jax.shard_map(
        per_device, mesh=mesh, in_specs=in_specs, out_specs=out_specs, check_vma=False
    )
```

profile of v0, /device:TPU:0, one launch (start us, length us, event | category | flops | bytes accessed | tf_op | source)
XLA Modules:
  0.0 291.8 jit_solution(2435914263683252794)
XLA Ops:
  0.6 0.7 broadcast_multiply_fusion.1
  1.4 0.8 copy.38
  2.4 0.8 copy.42
  4.2 2.4 scatter_custom_fusion
  6.7 5.0 %gather_fusion = s32[768]{0:T(1024)S(1)} fusion(s32[512]{0:T(512)S(1)} %reshape.271, s32[1024]{0:T(1024)S(1)} %pad_clamp_fusion.1), kind=kCustom, calls=%fused_computation | custom fusion | bytes 9216 | tf_op jit(solution)/shard_map/gather | solution.py:109
  11.7 0.8 all_to_all.9
  12.5 11.2 %all-to-all-start = ((s32[128,1,6]{2,1,0:T(1,128)}), s32[128,1,6]{2,1,0:T(1,128)S(1)}, u32[]{:S(2)}, u32[]{:S(2)}) async-start(s32[128,1,6]{2,1,0:T(1,128)} %bitcast.5), calls=%async_computation | async-start | bytes 131072 | tf_op jit(solution)/shard_map/all_to_all | solution.py:118
  23.7 2.5 reshape.272
  26.3 4.9 %copy.65 = f32[4,16,16,8,16]{4,2,0,3,1:T(8,128)} copy(f32[4,16,16,8,16]{4,3,2,1,0:T(8,128)} %reshape.272) | data formatting | bytes 1048576 | tf_op jit(solution)/shard_map/reshape | solution.py:86
  31.2 4.7 %reshape.273 = f32[128,1024]{1,0:T(8,128)S(1)} reshape(f32[16,8,4,16,16]{4,3,2,1,0:T(8,128)} %bitcast.94) | data formatting | bytes 1048576 | tf_op jit(solution)/shard_map/reshape | solution.py:88
  35.9 3.6 %gather_fusion.1 = f32[768,1024]{1,0:T(8,128)} fusion(f32[128,1024]{1,0:T(8,128)S(1)} %reshape.273, s32[1024]{0:T(1024)S(1)} %pad_clamp_fusion), kind=kCustom, calls=%fused_computation.1 | custom fusion | bytes 6294528 | tf_op jit(solution)/shard_map/gather | solution.py:108
  39.5 4.6 %gather.13 = f32[128,6,1024]{2,1,0:T(8,128)} reshape(f32[768,1024]{1,0:T(8,128)} %gather_fusion.1) | data formatting | bytes 6291456 | tf_op jit(solution)/shard_map/gather | solution.py:108
  44.5 5.0 %gather_fusion.2 = f32[768]{0:T(1024)S(1)} fusion(f32[512]{0:T(512)S(1)} %div.33, s32[1024]{0:T(1024)S(1)} %pad_clamp_fusion.1), kind=kCustom, calls=%fused_computation.2 | custom fusion | bytes 9216 | tf_op jit(solution)/shard_map/gather | solution.py:107
  49.7 4.5 %broadcast_multiply_fusion = f32[128,6,1024]{2,1,0:T(8,128)} fusion(f32[128,6,1024]{2,1,0:T(8,128)} %gather.13, f32[128,6]{1,0:T(8,128)S(1)} %mul.312), kind=kLoop, calls=%fused_computation.18 | loop fusion | flops 786432 | bytes 6294528 | tf_op jit(solution)/shard_map/mul | solution.py:108
  54.2 10.3 %all-to-all-start.1 = ((f32[128,6,1024]{2,1,0:T(8,128)}), f32[128,6,1024]{2,1,0:T(8,128)}, u32[]{:S(2)}, u32[]{:S(2)}) async-start(f32[128,6,1024]{2,1,0:T(8,128)} %broadcast_multiply_fusion), calls=%async_computation.1 | async-start | bytes 8388608 | tf_op jit(solution)/shard_map/all_to_all | solution.py:111
  67.7 49.8 %all-reduce = f32[32]{0:T(128)S(1)} all-reduce(f32[32]{0:T(128)S(1)} %get-tuple-element.640), channel_id=2, replica_groups=mesh['gx'=8,'gy'=16] {'gx'}, use_global_device_ids=true, to_apply=%add | all-reduce | flops 32 | bytes 256
  117.6 0.7 reshape.308
  118.3 40.3 %all-reduce.1 = f32[64]{0:T(128)S(1)} all-reduce(f32[64]{0:T(128)S(1)} %get-tuple-element.630), channel_id=5, replica_groups=mesh['gx'=8,'gy'=16] {'gy'}, use_global_device_ids=true, to_apply=%add.1 | all-reduce | flops 64 | bytes 512
  158.6 0.7 reshape.311
  160.7 0.7 multiply_exponential_fusion.2
  161.4 0.7 multiply_exponential_fusion
  162.6 0.8 reduce.6
  163.4 0.7 eq.63
  164.1 3.1 %reshape.274 = f32[768,1024]{1,0:T(8,128)S(1)} reshape(f32[128,6,1024]{2,1,0:T(8,128)} %all-to-all-done.1) | data formatting | bytes 6291456 | tf_op jit(solution)/shard_map/reshape | solution.py:126
  167.2 2.4 copy.46
  169.5 7.7 %convolution_bitcast_fusion = f32[4,16,16,8,16]{4,3,2,0,1:T(8,128)S(1)} fusion(f32[4,16,16,768,1]{3,2,1,0,4:T(8,128)} %bitcast.97, s32[768]{0:T(1024)} %eq.63, s32[16,8]{1,0:T(8,128)} %multiply_add_fusion), kind=kOutput, calls=%fused_computation.17 | convolution fusion | flops 1208057856 | bytes 3673600 | tf_op jit(solution)/shard_map/dot_general | solution.py:131
  177.2 2.2 copy.47
  179.4 3.3 %reshape.275 = f32[4,256,128]{2,1,0:T(8,128)S(1)} reshape(f32[4,16,16,8,16]{4,3,2,1,0:T(8,128)} %copy.47) | data formatting | bytes 1048576 | tf_op jit(solution)/shard_map/reshape | solution.py:135
  182.8 2.0 fusion.4
  184.8 11.3 %all-gather.1 = f32[32,1,128]{2,1,0:T(1,128)S(1)} all-gather(f32[4,1,128]{2,1,0:T(1,128)S(1)} %slice.31), channel_id=3, replica_groups=mesh['gx'=8,'gy'=16] {'gx'}, dimensions={0}, use_global_device_ids=true | all-gather | bytes 18432 | tf_op jit(solution)/shard_map/all_gather | solution.py:11
  196.1 5.7 %while.60 = (s32[]{:T(128)}, f32[4,128]{1,0:T(4,128)S(1)}, s32[]{:T(128)}, f32[8,4,1]{1,2,0:T(1,128)}, f32[8,4,128]{2,1,0:T(4,128)S(1)}, /*index=5*/s32[]{:T(128)}, s32[]{:T(128)}) while((s32[]{:T(128)}, f32[4,128]{1,0:T(4,128)S(1)}, s32[]{:T(128)}, f32[8,4,1]{1,2,0:T(1,128)}, f32[8,4,128]{2,1,0:T(4,128)S(1)}, ...), condition=%wide.region_6.7_spmd.clone, body=%wide.region_5.6_spmd.clone.sunk | while | flops 2052 | bytes 6305 | solution.py:24
  196.8 0.7 dynamic-slice_bitcast_fusion.8
  197.5 0.7 dynamic-slice_bitcast_fusion.8
  198.3 0.7 dynamic-slice_bitcast_fusion.8
  201.1 0.7 dynamic-slice_bitcast_fusion.8
  201.8 1.3 convolution_multiply_fusion
  203.2 11.7 %all-gather.2 = f32[32,1,128]{2,1,0:T(1,128)S(1)} all-gather(f32[4,1,128]{2,1,0:T(1,128)S(1)} %slice.32), channel_id=4, replica_groups=mesh['gx'=8,'gy'=16] {'gx'}, dimensions={0}, use_global_device_ids=true | all-gather | bytes 18432 | tf_op jit(solution)/shard_map/all_gather | solution.py:11
  214.9 5.7 %while.61 = (s32[]{:T(128)}, f32[4,128]{1,0:T(4,128)S(1)}, s32[]{:T(128)}, f32[8,4,1]{1,2,0:T(1,128)}, f32[8,4,128]{2,1,0:T(4,128)S(1)}, /*index=5*/s32[]{:T(128)}, s32[]{:T(128)}, s32[]{:T(128)}, s32[]{:T(128)}) while((s32[]{:T(128)}, f32[4,128]{1,0:T(4,128)S(1)}, s32[]{:T(128)}, f32[8,4,1]{1,2,0:T(1,128)}, ...), condition=%wide.region_8.9_spmd.clone, body=%wide.region_7.8_spmd.clone.sunk | while | flops 2056 | bytes 6367 | solution.py:24
  214.9 0.7 dynamic-slice_bitcast_fusion.9
  217.7 0.7 dynamic-slice_bitcast_fusion.9
  218.4 0.7 dynamic-slice_bitcast_fusion.9
  219.2 0.7 dynamic-slice_bitcast_fusion.9
  220.6 0.8 fusion.7
  221.4 20.4 %all-gather.4 = f32[64,256,1]{1,2,0:T(1,128)S(1)} all-gather(f32[4,256,1]{1,2,0:T(1,128)S(1)} %slice.33), channel_id=6, replica_groups=mesh['gx'=8,'gy'=16] {'gy'}, dimensions={0}, use_global_device_ids=true | all-gather | bytes 69632 | tf_op jit(solution)/shard_map/all_gather | solution.py:11
  242.0 11.6 %while.62 = (s32[]{:T(128)}, f32[4,256]{1,0:T(4,128)S(1)}, s32[]{:T(128)}, f32[16,4,1]{1,2,0:T(1,128)}, f32[16,4,256]{2,1,0:T(4,128)S(1)}, /*index=5*/s32[]{:T(128)}, s32[]{:T(128)}) while((s32[]{:T(128)}, f32[4,256]{1,0:T(4,128)S(1)}, s32[]{:T(128)}, f32[16,4,1]{1,2,0:T(1,128)}, f32[16,4,256]{2,1,0:T(4,128)S(1)}, ...), condition=%wide.region_10.11_spmd.clone, body=%wide.region_9.10_spmd.clone.sunk | while | flops 4100 | bytes 12449 | solution.py:24
  243.4 0.7 dynamic-slice_bitcast_fusion.10
  245.6 0.7 dynamic-slice_bitcast_fusion.10
  247.0 0.7 dynamic-slice_bitcast_fusion.10
  247.8 0.7 dynamic-slice_bitcast_fusion.10
  249.2 0.7 dynamic-slice_bitcast_fusion.10
  250.6 0.7 dynamic-slice_bitcast_fusion.10
  251.4 0.7 dynamic-slice_bitcast_fusion.10
  253.6 1.1 convolution_multiply_fusion.1
  254.9 24.2 %all-gather.5 = f32[64,256,1]{1,2,0:T(1,128)S(1)} all-gather(f32[4,256,1]{1,2,0:T(1,128)S(1)} %copy.55), channel_id=7, replica_groups=mesh['gx'=8,'gy'=16] {'gy'}, dimensions={0}, use_global_device_ids=true | all-gather | bytes 69632 | tf_op jit(solution)/shard_map/all_gather | solution.py:11
  279.2 11.6 %while.63 = (s32[]{:T(128)}, f32[4,256]{1,0:T(4,128)S(1)}, s32[]{:T(128)}, f32[16,4,1]{1,2,0:T(1,128)}, f32[16,4,256]{2,1,0:T(4,128)S(1)}, /*index=5*/s32[]{:T(128)}, s32[]{:T(128)}, s32[]{:T(128)}, s32[]{:T(128)}) while((s32[]{:T(128)}, f32[4,256]{1,0:T(4,128)S(1)}, s32[]{:T(128)}, f32[16,4,1]{1,2,0:T(1,128)}, ...), condition=%wide.region_12.13_spmd.clone, body=%wide.region_11.12_spmd.clone.sunk | while | flops 4104 | bytes 12511 | solution.py:24
  280.7 0.7 dynamic-slice_bitcast_fusion.11
  281.4 0.7 dynamic-slice_bitcast_fusion.11
  282.9 0.7 dynamic-slice_bitcast_fusion.11
  284.3 0.7 dynamic-slice_bitcast_fusion.11
  285.0 0.7 dynamic-slice_bitcast_fusion.11
  285.8 0.6 dynamic-slice_bitcast_fusion.11
  286.5 0.7 dynamic-slice_bitcast_fusion.11
  288.7 0.7 dynamic-slice_bitcast_fusion.11
  290.8 1.0 add_add_fusion
  (162 shorter events, 25.3 us)
Async XLA Ops:
  0.6 23.0 %copy-start.10 = (s32[1,1,128,4]{2,3,1,0:T(4,128)S(1)}, s32[1,1,128,4]{2,3,1,0:T(4,128)}, u32[]{:S(2)}) copy-start(s32[1,1,128,4]{2,3,1,0:T(4,128)} %param.20) | copy-start | bytes 6148
  0.6 23.1 %copy-start.1 = (f32[4,256,128]{2,1,0:T(8,128)S(1)}, f32[4,256,128]{2,1,0:T(8,128)}, u32[]{:S(2)}) copy-start(f32[4,256,128]{2,1,0:T(8,128)} %param.15) | copy-start | bytes 1572868
  12.5 41.7 %all-to-all-start = ((s32[128,1,6]{2,1,0:T(1,128)}), s32[128,1,6]{2,1,0:T(1,128)S(1)}, u32[]{:S(2)}, u32[]{:S(2)}) async-start(s32[128,1,6]{2,1,0:T(1,128)} %bitcast.5), calls=%async_computation | async-start | bytes 131072 | tf_op jit(solution)/shard_map/all_to_all | solution.py:118
  54.2 10.4 %copy-start.15 = (u32[128]{0:T(128)S(1)}, u32[128]{0:T(128)}, u32[]{:S(2)}) copy-start(u32[128]{0:T(128)} %constant.199) | copy-start | bytes 1540
  54.2 11.0 %copy-start.14 = (u32[128]{0:T(128)S(1)}, u32[128]{0:T(128)}, u32[]{:S(2)}) copy-start(u32[128]{0:T(128)} %constant.194) | copy-start | bytes 1540
  54.2 12.9 %copy-start.13 = (f32[4]{0:T(128)S(1)}, f32[4]{0:T(128)}, u32[]{:S(2)}) copy-start(f32[4]{0:T(128)} %param.21) | copy-start | bytes 52
  54.2 109.9 %all-to-all-start.1 = ((f32[128,6,1024]{2,1,0:T(8,128)}), f32[128,6,1024]{2,1,0:T(8,128)}, u32[]{:S(2)}, u32[]{:S(2)}) async-start(f32[128,6,1024]{2,1,0:T(8,128)} %broadcast_multiply_fusion), calls=%async_computation.1 | async-start | bytes 8388608 | tf_op jit(solution)/shard_map/all_to_all | solution.py:111
  67.7 94.3 %copy-start.5 = (f32[4]{0:T(128)}, f32[4]{0:T(128)S(1)}, u32[]{:S(2)}) copy-start(f32[4]{0:T(128)S(1)} %get-tuple-element.641) | copy-start | bytes 52
  179.4 3.3 %copy-start.3 = (f32[4,256,128]{2,1,0:T(8,128)S(1)}, f32[4,256,128]{2,1,0:T(8,128)}, u32[]{:S(2)}) copy-start(f32[4,256,128]{2,1,0:T(8,128)} %param.16) | copy-start | bytes 1572868
  179.4 3.4 %copy-start.6 = (f32[4]{0:T(128)S(1)}, f32[4]{0:T(128)}, u32[]{:S(2)}) copy-start(f32[4]{0:T(128)} %copy-done.5) | copy-start | bytes 52
  179.4 22.4 %copy-start.11 = (f32[4,256]{1,0:T(4,128)S(1)}, f32[4,256]{1,0:T(4,128)}, u32[]{:S(2)}) copy-start(f32[4,256]{1,0:T(4,128)} %get-tuple-element.638) | copy-start | bytes 12292
  179.4 22.4 %copy-start.12 = (f32[4]{0:T(128)S(1)}, f32[4]{0:T(128)}, u32[]{:S(2)}) copy-start(f32[4]{0:T(128)} %get-tuple-element.639) | copy-start | bytes 52
  179.4 41.2 %copy-start.4 = (pred[128,128]{0,1:T(8,128)(4,1)S(1)}, pred[128,128]{0,1:T(8,128)(4,1)}, u32[]{:S(2)}) copy-start(pred[128,128]{0,1:T(8,128)(4,1)} %fusion.47) | copy-start | bytes 49156
  179.4 41.1 %copy-start.7 = (f32[4,256]{1,0:T(4,128)S(1)}, f32[4,256]{1,0:T(4,128)}, u32[]{:S(2)}) copy-start(f32[4,256]{1,0:T(4,128)} %get-tuple-element.637) | copy-start | bytes 12292
  182.8 109.0 %copy-start = (f32[4,256,128]{2,1,0:T(8,128)}, f32[4,256,128]{2,1,0:T(8,128)S(1)}, u32[]{:S(2)}) copy-start(f32[4,256,128]{2,1,0:T(8,128)S(1)} %reshape.275) | copy-start | bytes 1572868
  182.8 70.8 %copy-start.9 = (f32[4,128]{1,0:T(4,128)S(1)}, f32[4,128]{1,0:T(4,128)}, u32[]{:S(2)}) copy-start(f32[4,128]{1,0:T(4,128)} %get-tuple-element.636) | copy-start | bytes 6148
  182.8 108.0 %copy-start.2 = (f32[4,256,128]{2,1,0:T(8,128)S(1)}, f32[4,256,128]{2,1,0:T(8,128)}, u32[]{:S(2)}) copy-start(f32[4,256,128]{2,1,0:T(8,128)} %param.17) | copy-start | bytes 1572868
  182.8 108.0 %copy-start.8 = (f32[4,128]{1,0:T(4,128)S(1)}, f32[4,128]{1,0:T(4,128)}, u32[]{:S(2)}) copy-start(f32[4,128]{1,0:T(4,128)} %get-tuple-element.635) | copy-start | bytes 6148
where the time goes:
time: 293 us; the launch traced here: 292 us
  blocking collectives  158 us (54%)
  local copies, waits for them, and re-layouts  82 us (28%)
  starting transfers between devices  21.5 us (7%)
  other arithmetic  15.2 us (5%)
  matrix products  13 us (4%)
    unnamed x2, blocking collectives  90.2 us
    all_gather x4, blocking collectives, entering_2(): everything = jax.tree.map(lambda part: lax.all_gather(part, axis), array)  67.5 us
    mul x48, local copies, waits for them, and re-layouts, compose(): return (former[0] * latter[0], latter[0] * former[1] + latter[1])  30.6 us
    all_to_all x1, starting transfers between devices, per_device(): lax.all_to_all(labels.reshape(device_count, capacity), ('gx', 'gy'), spli...  11.2 us
    all_to_all x1, starting transfers between devices, per_device(): lax.all_to_all(outgoing.reshape(device_count, capacity, tile_cells), ('gx...  10.3 us
    gather x2, local copies, waits for them, and re-layouts, per_device(): outgoing = tiles[owner_safe // fanout] * weights[:, None]  8.24 us
    dot_general x1, matrix products, per_device(): pushed_tiles = jnp.dot(collect, arrived, precision=lax.Precision.HIGHEST)  7.66 us
    reshape x2, local copies, waits for them, and re-layouts, per_device(): source_mass.reshape(planes, tiles_x, TS, tiles_y, TS)  7.45 us
  transfers between devices with their start and end apart: 2, of which 0 were waited for; matrix products, arithmetic and copies ran while one was open for 13% of the time, Pallas kernels for 0%

commit v1 on v0

v1 whole, which is shorter than its diff:
```python
import functools
import jax
import jax.numpy as jnp
from jax import lax
from jax.experimental import pallas as pl
from jax.experimental.pallas import tpu as pltpu
from jax.sharding import PartitionSpec as P

MESH = pl.DeviceIdType.MESH
TS = 16
SLOTS = 6
LANES = 128
STEP = 37
CHUNKS = 4
F32 = jnp.float32
BF16 = jnp.bfloat16


def split2(a):
    hi = a.astype(BF16)
    return hi, (a - hi.astype(F32)).astype(BF16)


def split3(a):
    hi = a.astype(BF16)
    rest = a - hi.astype(F32)
    mid = rest.astype(BF16)
    return hi, mid, (rest - mid.astype(F32)).astype(BF16)


def dot(a, b, dims=((1,), (0,))):
    return lax.dot_general(a, b, (dims, ((), ())), preferred_element_type=F32)


def dot3(a, b, dims=((1,), (0,))):
    ah, al = a
    bh, bl = b
    return dot(ah, bh, dims) + (dot(ah, bl, dims) + dot(al, bh, dims))


def dot_f32(a, b, dims=((1,), (0,))):
    return lax.dot_general(
        a, b, (dims, ((), ())), precision=lax.Precision.HIGHEST, preferred_element_type=F32
    )


def iota(shape, axis):
    return lax.broadcasted_iota(jnp.int32, shape, axis)


def block_transpose(vectors):
    lane_block = iota((8, LANES), 1) // TS
    vectors = list(vectors)
    for bit in (4, 2, 1):
        low = (lane_block & bit) == 0
        result = [None] * 8
        for a in range(8):
            if a & bit:
                continue
            b = a | bit
            up, down = vectors[a], vectors[b]
            result[a] = jnp.where(low, up, pltpu.roll(down, bit * TS, 1))
            result[b] = jnp.where(low, pltpu.roll(up, LANES - bit * TS, 1), down)
        vectors = result
    return vectors


def displaced(p, q, row):
    shift = (row * STEP) & 127
    dp, dq = shift >> 4, shift & 15
    tp = ((((p >> 1) + (dp >> 1)) & 3) << 1) + (((p & 1) + (dp & 1)) & 1)
    tq = ((((q >> 2) + (dq >> 2)) & 3) << 2) + (((q & 3) + (dq & 3)) & 3)
    return tp, tq


def powers(logs, exponent):
    return jnp.exp(exponent.astype(F32) * logs)


def kernel(
    source_ref, target_ref, potential_ref, device_ref, tile_ref, count_ref, reach_ref,
    pushed_ref, next_ref,
    natural, tiles, packed, packed_labels, arrived, arrived_labels, gathered,
    target, potential, xtab_hi, xtab_lo, ytab_hi, ytab_lo, xmsg, xall, ymsg, yall, smooth,
    load_sem, self_sem, send_sem, recv_sem, label_send, label_recv, store_sem,
    x_send, x_recv, y_send, y_recv,
):
    p, q = lax.axis_index("gx"), lax.axis_index("gy")
    devices, n_gx, n_gy = 128, 8, 16
    planes, cx, cy = source_ref.shape
    tile_rows, tile_cols = cx // TS, cy // TS
    rows_per = SLOTS * 8

    load = pltpu.make_async_copy(source_ref, natural, load_sem.at[0])
    load.start()
    load_target = pltpu.make_async_copy(target_ref, target, load_sem.at[1])
    load_target.start()
    load_potential = pltpu.make_async_copy(potential_ref, potential, load_sem.at[2])
    load_potential.start()

    barrier = pltpu.get_barrier_semaphore()

    def greet(row, carry):
        pl.semaphore_signal(barrier, inc=1, device_id=displaced(p, q, row), device_id_type=MESH)
        return carry

    lax.fori_loop(1, devices, greet, 0)

    names = device_ref[...]
    places = tile_ref[...].astype(F32)
    counts = count_ref[...].astype(F32)
    shares = counts / jnp.sum(counts, axis=0, keepdims=True)
    row_p, row_q = displaced(p, q, iota((devices, LANES), 0))
    owner = row_p * n_gy + row_q
    named = jnp.zeros((devices, LANES), F32)
    share = jnp.zeros((devices, LANES), F32)
    place = jnp.zeros((devices, LANES), F32)
    for j in range(names.shape[0]):
        match = (owner == names[j : j + 1, :]).astype(F32)
        named += match
        share += match * shares[j : j + 1, :]
        place += match * places[j : j + 1, :]
    earlier = (iota((LANES, LANES), 0) < iota((LANES, LANES), 1)).astype(BF16)
    rank = dot(named.astype(BF16), earlier)
    lane = iota((devices, LANES), 1)
    labels = jnp.zeros((devices, LANES), F32)
    picks, weights = [], []
    for k in range(SLOTS):
        pick = jnp.where(rank == float(k), named, 0.0)
        picks.append(pick.astype(BF16))
        weights.append(jnp.sum(pick * share, axis=1, keepdims=True))
        label = jnp.sum(pick * place, axis=1, keepdims=True)
        labels = jnp.where(lane == k, label, labels)
    packed_labels[...] = labels[:, None, :]

    load.wait()
    for xo in range(tile_rows):
        parts = [
            natural[g // 2, pl.ds(xo * TS + (g % 2) * 8, 8), :] for g in range(2 * planes)
        ]
        for yo, value in enumerate(block_transpose(parts)):
            tiles[pl.ds((xo * tile_cols + yo) * 8, 8), :] = value
    parts = []
    for c in range(8):
        parts.append(split3(tiles[pl.ds(c, LANES, stride=8), :]))

    chunk = devices // CHUNKS
    for g in range(CHUNKS):
        pick = jnp.concatenate([a[g * chunk : (g + 1) * chunk] for a in picks], axis=0)
        pick3 = jnp.concatenate([pick, pick, pick], axis=1)
        for c in range(8):
            value = dot(pick3, jnp.concatenate(parts[c], axis=0))
            for k in range(SLOTS):
                packed[pl.ds(g * chunk * rows_per + k * 8 + c, chunk, stride=rows_per), :] = (
                    value[k * chunk : (k + 1) * chunk] * weights[k][g * chunk : (g + 1) * chunk]
                )
        if g == 0:
            pl.semaphore_wait(barrier, devices - 1)

        def send(row, carry):
            to = displaced(p, q, row)
            start = pl.multiple_of(row * rows_per, 8)
            pltpu.make_async_remote_copy(
                src_ref=packed.at[pl.ds(start, rows_per)],
                dst_ref=arrived.at[pl.ds(start, rows_per)],
                send_sem=send_sem,
                recv_sem=recv_sem.at[g],
                device_id=to,
                device_id_type=MESH,
            ).start()
            pltpu.make_async_remote_copy(
                src_ref=packed_labels.at[row],
                dst_ref=arrived_labels.at[row],
                send_sem=label_send,
                recv_sem=label_recv,
                device_id=to,
                device_id_type=MESH,
            ).start()
            return carry

        lax.fori_loop(max(g * chunk, 1), (g + 1) * chunk, send, 0)
    own = pltpu.make_async_copy(
        packed.at[pl.ds(0, rows_per)], arrived.at[pl.ds(0, rows_per)], self_sem.at[0]
    )
    own.start()
    own_label = pltpu.make_async_copy(packed_labels.at[0], arrived_labels.at[0], self_sem.at[1])
    own_label.start()

    decay = [1.0 - 1.0 / reach_ref[z] for z in range(planes)]
    decay = [jnp.full((1, 1), d, F32) for d in decay]
    logs = [jnp.log(d) for d in decay]
    scale = [(1.0 - d) ** 2 for d in decay]

    def tables(z, n):
        gap = iota((n, n), 0) - iota((n, n), 1)
        lower = jnp.where(gap >= 0, powers(logs[z], jnp.maximum(gap, 0)), 0.0)
        both = scale[z] * dot_f32(lower, lower, ((0,), (0,)))
        return both

    for z in range(planes):
        hi, lo = split2(tables(z, cx))
        xtab_hi[z], xtab_lo[z] = hi, lo
        hi, lo = split2(tables(z, cy))
        ytab_hi[z], ytab_lo[z] = hi, lo

    def edges(z, n):
        at = iota((1, n), 1)
        last = powers(logs[z], n - 1 - at)
        rise = powers(logs[z], at + 1)
        fall = powers(logs[z], n - at)
        gap = iota((n, n), 0) - iota((n, n), 1)
        lower = jnp.where(gap >= 0, powers(logs[z], jnp.maximum(gap, 0)), 0.0)
        swept = scale[z] * dot_f32(jnp.broadcast_to(rise, (8, n)), lower)[0:1]
        return last, swept, fall

    x_edges = [edges(z, cx) for z in range(planes)]
    y_edges = [edges(z, cy) for z in range(planes)]

    def whole(ref, first, count, sem):
        part = ref.at[pl.ds(first, count)]
        pltpu.make_async_copy(part, part, sem).wait()

    own.wait()
    own_label.wait()
    whole(arrived_labels, 1, devices - 1, label_recv)
    label_lanes = jnp.transpose(arrived_labels[...].reshape(devices, LANES))
    tile_index = iota((LANES, LANES), 0).astype(F32)
    wanted = [(label_lanes[k : k + 1, :] == tile_index).astype(BF16) for k in range(SLOTS)]
    sums = [jnp.zeros((LANES, LANES), F32) for _ in range(8)]
    for g in range(CHUNKS):
        first = 1 if g == 0 else g * chunk
        whole(arrived, first * rows_per, ((g + 1) * chunk - first) * rows_per, recv_sem.at[g])
        select = jnp.concatenate([w[:, g * chunk : (g + 1) * chunk] for w in wanted], axis=1)
        for c in range(8):
            rows = jnp.concatenate(
                [
                    arrived[pl.ds(g * chunk * rows_per + k * 8 + c, chunk, stride=rows_per), :]
                    for k in range(SLOTS)
                ],
                axis=0,
            )
            hi, mid, lo = split3(rows)
            sums[c] = sums[c] + (dot(select, hi) + (dot(select, mid) + dot(select, lo)))
    for c in range(8):
        tiles[pl.ds(c, LANES, stride=8), :] = sums[c]
    for xo in range(tile_rows):
        parts = [tiles[pl.ds((xo * tile_cols + yo) * 8, 8), :] for yo in range(tile_cols)]
        for g, value in enumerate(block_transpose(parts)):
            gathered[g // 2, pl.ds(xo * TS + (g % 2) * 8, 8), :] = value
    store_pushed = pltpu.make_async_copy(gathered, pushed_ref, store_sem.at[0])
    store_pushed.start()

    load_target.wait()
    row8 = iota((8, 1), 0)
    ends = jnp.zeros((8, cy), F32)
    for z in range(planes):
        mismatch = target[z] - gathered[z]
        m2 = split2(mismatch)
        base = dot3((xtab_hi[z], xtab_lo[z]), m2)
        smooth[z] = base
        weights8 = jnp.where(row8 == z, x_edges[z][0], 0.0)
        ends += dot_f32(weights8, mismatch)
        ends += jnp.where(row8 == planes + z, base[0:1], 0.0)
    xmsg[...] = ends

    def line_peer(i):
        return ((((p >> 1) + (i >> 1)) & 3) << 1) + (((p & 1) + (i & 1)) & 1)

    def send_x(i, carry):
        pltpu.make_async_remote_copy(
            src_ref=xmsg, dst_ref=xall.at[p], send_sem=x_send, recv_sem=x_recv,
            device_id=(line_peer(i), q), device_id_type=MESH,
        ).start()
        return carry

    lax.fori_loop(1, n_gx, send_x, 0)
    xall[p] = ends
    xmsg_done = pltpu.make_async_copy(
        xall.at[pl.ds(0, n_gx - 1)], xall.at[pl.ds(0, n_gx - 1)], x_recv
    )
    xmsg_done.wait()

    def boundary(all_ref, count, here, across, first_swept, width):
        low = row8 < planes
        entering = jnp.zeros((8, width), F32)
        entry, picked = [], jnp.zeros((8, width), F32)
        for i in range(count):
            entry.append(entering)
            picked = jnp.where(here == i, entering, picked)
            entering = jnp.where(low, across * entering + all_ref[i], 0.0)
        leaving = jnp.zeros((8, width), F32)
        out = jnp.zeros((8, width), F32)
        for i in reversed(range(count)):
            out = jnp.where(here == i, leaving, out)
            begun = all_ref[i] + pltpu.roll(first_swept * entry[i], planes, 0)
            leaving = jnp.where(low, 0.0, across * leaving + begun)
        return picked + out

    def column8(values):
        result = jnp.zeros((8, 1), F32)
        for z, v in enumerate(values):
            result = jnp.where((row8 == z) | (row8 == planes + z), v, result)
        return result

    across_x = column8([powers(logs[z], jnp.full((1, 1), cx, jnp.int32)) for z in range(planes)])
    across_y = column8([powers(logs[z], jnp.full((1, 1), cy, jnp.int32)) for z in range(planes)])
    swept_x = column8([x_edges[z][1][:, 0:1] for z in range(planes)])
    swept_y = column8([y_edges[z][1][:, 0:1] for z in range(planes)])

    def spread(z, edge):
        return jnp.where(row8 == z, edge[1], 0.0) + jnp.where(row8 == planes + z, edge[2], 0.0)

    inflow = boundary(xall, n_gx, p, across_x, swept_x, cy)
    ends = jnp.zeros((8, cx), F32)
    for z in range(planes):
        value = smooth[z] + dot_f32(spread(z, x_edges[z]), inflow, ((0,), (0,)))
        smooth[z] = value
        start_row = ytab_hi[z][0:1].astype(F32) + ytab_lo[z][0:1].astype(F32)
        weights8 = jnp.where(row8 == z, y_edges[z][0], 0.0) + jnp.where(
            row8 == planes + z, start_row, 0.0
        )
        ends += dot_f32(weights8, value, ((1,), (1,)))
    ymsg[...] = ends

    def send_y(i, carry):
        to = ((((q >> 2) + (i >> 2)) & 3) << 2) + (((q & 3) + (i & 3)) & 3)
        pltpu.make_async_remote_copy(
            src_ref=ymsg, dst_ref=yall.at[q], send_sem=y_send, recv_sem=y_recv,
            device_id=(p, to), device_id_type=MESH,
        ).start()
        return carry

    lax.fori_loop(1, n_gy, send_y, 0)
    yall[q] = ends
    load_potential.wait()
    for z in range(planes):
        potential[z] = potential[z] + dot3(split2(smooth[z]), (ytab_hi[z], ytab_lo[z]))
    part = yall.at[pl.ds(0, n_gy - 1)]
    pltpu.make_async_copy(part, part, y_recv).wait()
    inflow = boundary(yall, n_gy, q, across_y, swept_y, cx)
    for z in range(planes):
        potential[z] = potential[z] + dot_f32(inflow, spread(z, y_edges[z]), ((0,), (0,)))
    store_next = pltpu.make_async_copy(potential, next_ref, store_sem.at[1])
    store_next.start()

    whole(packed, rows_per, (devices - 1) * rows_per, send_sem)
    whole(packed_labels, 1, devices - 1, label_send)
    whole(xall, 0, n_gx - 1, x_send)
    whole(yall, 0, n_gy - 1, y_send)
    store_pushed.wait()
    store_next.wait()


def per_device(source_mass, target_density, potential, dest_device, dest_tile, mass_counts, reach):
    planes, cx, cy = source_mass.shape

    def lanes(a):
        return jnp.swapaxes(a.reshape(a.shape[2:]), 0, 1)

    rows = LANES * SLOTS * 8
    hbm = pl.BlockSpec(memory_space=pl.ANY)
    vmem = pl.BlockSpec(memory_space=pltpu.VMEM)
    dma = pltpu.SemaphoreType.DMA
    grid = jax.ShapeDtypeStruct((planes, cx, cy), F32)
    return pl.pallas_call(
        kernel,
        out_shape=(grid, grid),
        in_specs=[hbm, hbm, hbm, vmem, vmem, vmem, pl.BlockSpec(memory_space=pltpu.SMEM)],
        out_specs=(hbm, hbm),
        scratch_shapes=[
            pltpu.VMEM((planes, cx, cy), F32),
            pltpu.VMEM((LANES * 8, LANES), F32),
            pltpu.VMEM((rows, LANES), F32),
            pltpu.VMEM((LANES, 1, LANES), F32),
            pltpu.VMEM((rows, LANES), F32),
            pltpu.VMEM((LANES, 1, LANES), F32),
            pltpu.VMEM((planes, cx, cy), F32),
            pltpu.VMEM((planes, cx, cy), F32),
            pltpu.VMEM((planes, cx, cy), F32),
            pltpu.VMEM((planes, cx, cx), BF16),
            pltpu.VMEM((planes, cx, cx), BF16),
            pltpu.VMEM((planes, cy, cy), BF16),
            pltpu.VMEM((planes, cy, cy), BF16),
            pltpu.VMEM((8, cy), F32),
            pltpu.VMEM((8, 8, cy), F32),
            pltpu.VMEM((8, cx), F32),
            pltpu.VMEM((16, 8, cx), F32),
            pltpu.VMEM((planes, cx, cy), F32),
            dma((3,)),
            dma((2,)),
            dma,
            dma((CHUNKS,)),
            dma,
            dma,
            dma((2,)),
            dma,
            dma,
            dma,
            dma,
        ],
        compiler_params=pltpu.CompilerParams(
            collective_id=0, has_side_effects=True, vmem_limit_bytes=48 * 1024 * 1024
        ),
        name="dual_step",
    )(
        source_mass, target_density, potential,
        lanes(dest_device), lanes(dest_tile), lanes(mass_counts), reach,
    )


def solution(mesh):
    in_specs = (
        P(None, "gx", "gy"),
        P(None, "gx", "gy"),
        P(None, "gx", "gy"),
        P("gx", "gy", None, None),
        P("gx", "gy", None, None),
        P("gx", "gy", None, None),
        P(),
    )
    out_specs = (P(None, "gx", "gy"), P(None, "gx", "gy"))
    return jax.shard_map(
        per_device, mesh=mesh, in_specs=in_specs, out_specs=out_specs, check_vma=False
    )
```

time: 293 us -> 73.5 us (0.25)
  blocking collectives: 158 us -> 0 us
  local copies, waits for them, and re-layouts: 82 us -> 6.07 us
  Pallas kernels: 0 us -> 66.5 us
  starting transfers between devices: 21.5 us -> 0 us
  other arithmetic: 15.2 us -> 0 us
  matrix products: 13 us -> 0 us
    unnamed x2 -> x0, blocking collectives: 90.2 us -> none
    all_gather x4 -> x0, blocking collectives: 67.5 us -> none  [entering_2(): everything = jax.tree.map(lambda part: lax.all_gather(part, axis), array)]
    pallas_call x0 -> x1, Pallas kernels: none -> 66.5 us  [per_device(): pl.pallas_call(kernel, out_shape=(grid, grid), in_specs=[hbm, hbm, hbm, v...]
    mul x51 -> x0, local copies, waits for them, and re-layouts: 30.9 us -> none  [the longest x48 30.6 us: compose(): return (former[0] * latter[0], latter[0] * former[1] + latter[1])]
    all_to_all x2 -> x0, starting transfers between devices: 21.5 us -> none  [the longest x1 11.2 us: per_device(): lax.all_to_all(labels.reshape(device_count, capacity), ('gx', 'gy'), spli...]
    reshape x6 -> x0, local copies, waits for them, and re-layouts: 18.6 us -> none  [the longest x2 7.45 us: per_device(): source_mass.reshape(planes, tiles_x, TS, tiles_y, TS)]
    gather x4 -> x0, local copies, waits for them, and re-layouts: 18.3 us -> none  [the longest x2 8.24 us: per_device(): outgoing = tiles[owner_safe // fanout] * weights[:, None]]
    dot_general x5 -> x0, matrix products: 13 us -> none  [the longest x1 7.66 us: per_device(): pushed_tiles = jnp.dot(collect, arrived, precision=lax.Precision.HIGHEST)]
  transfers between devices with their start and end apart: 2 -> 0, of which waited for: 0 -> 0; matrix products, arithmetic and copies ran while one was open for 13% -> 0% of each run, Pallas kernels for 0% -> 0%
where the time goes in v1:
time: 73.5 us; the launch traced here: 73.2 us
  Pallas kernels  66.5 us (90%)
  local copies, waits for them, and re-layouts  6.07 us (8%)
    pallas_call x1, Pallas kernels, per_device(): pl.pallas_call(kernel, out_shape=(grid, grid), in_specs=[hbm, hbm, hbm, v...  66.5 us
    unnamed x16, local copies, waits for them, and re-layouts  6.07 us

profile of v1, /device:TPU:0, one launch (start us, length us, event | category | flops | bytes accessed | tf_op | source)
XLA Modules:
  0.0 73.2 jit_solution(2703945411176632272)
XLA Ops:
  0.6 0.0 copy-start.4
  0.6 0.0 copy-start.3
  0.7 0.0 copy-start.6
  0.7 0.7 copy-done.4
  1.3 0.0 copy-done.3
  1.3 0.0 copy-done.6
  1.3 0.0 copy-start
  1.3 1.0 %copy-done = f32[4,256,128]{2,1,0:T(8,128)S(1)} copy-done((f32[4,256,128]{2,1,0:T(8,128)S(1)}, f32[4,256,128]{2,1,0:T(8,128)}, u32[]{:S(2)}) %copy-start) | copy-done | bytes 524312
  2.4 0.0 copy-start.1
  2.4 1.0 %copy-done.1 = f32[4,256,128]{2,1,0:T(8,128)S(1)} copy-done((f32[4,256,128]{2,1,0:T(8,128)S(1)}, f32[4,256,128]{2,1,0:T(8,128)}, u32[]{:S(2)}) %copy-start.1) | copy-done | bytes 524312
  3.4 0.0 copy-start.2
  3.4 1.0 %copy-done.2 = f32[4,256,128]{2,1,0:T(8,128)S(1)} copy-done((f32[4,256,128]{2,1,0:T(8,128)S(1)}, f32[4,256,128]{2,1,0:T(8,128)}, u32[]{:S(2)}) %copy-start.2) | copy-done | bytes 524312
  4.5 0.0 copy-start.5
  4.5 0.7 copy-done.5
  5.1 66.5 %dual_step.1 = (f32[4,256,128]{2,1,0:T(8,128)S(1)}, f32[4,256,128]{2,1,0:T(8,128)S(1)}) custom-call(f32[4,256,128]{2,1,0:T(8,128)S(1)} %copy-done, f32[4,256,128]{2,1,0:T(8,128)S(1)} %copy-done.1, f32[4,256,128]{2,1,0:T(8,128)S(1)} %copy-done.2, s32[4,128]{1,0:T(4,128)S(1)} %bitcast.9, s32[4,128]{1,0:T(4,128)S(1)} %bitcast.10, s32[4,128]{1,0:T(4,128)S(1)} %bitcast.11, ...), custom_call_target="tpu_custom_call" | custom-call | tf_op jit(solution)/shard_map/dual_step/pallas_call | solution.py:365
  71.6 0.8 %copy.11 = f32[4,256,128]{2,1,0:T(8,128)} copy(f32[4,256,128]{2,1,0:T(8,128)S(1)} %get-tuple-element.4) | data formatting | bytes 1048576
  72.4 0.8 %copy.12 = f32[4,256,128]{2,1,0:T(8,128)} copy(f32[4,256,128]{2,1,0:T(8,128)S(1)} %get-tuple-element.5) | data formatting | bytes 1048576
Async XLA Ops:
  0.6 0.7 copy-start.4
  0.6 0.7 copy-start.3
  0.7 0.7 copy-start.6
  1.3 1.0 %copy-start = (f32[4,256,128]{2,1,0:T(8,128)S(1)}, f32[4,256,128]{2,1,0:T(8,128)}, u32[]{:S(2)}) copy-start(f32[4,256,128]{2,1,0:T(8,128)} %source_ref.1) | copy-start | bytes 1572868
  2.4 1.0 %copy-start.1 = (f32[4,256,128]{2,1,0:T(8,128)S(1)}, f32[4,256,128]{2,1,0:T(8,128)}, u32[]{:S(2)}) copy-start(f32[4,256,128]{2,1,0:T(8,128)} %target_ref.1) | copy-start | bytes 1572868
  3.4 1.0 %copy-start.2 = (f32[4,256,128]{2,1,0:T(8,128)S(1)}, f32[4,256,128]{2,1,0:T(8,128)}, u32[]{:S(2)}) copy-start(f32[4,256,128]{2,1,0:T(8,128)} %potential_ref.1) | copy-start | bytes 1572868
  4.5 0.7 copy-start.5

commit v2 on v1

v2 whole, which is shorter than its diff:
```python
import jax
import jax.numpy as jnp
from jax import lax
from jax.experimental import pallas as pl
from jax.experimental.pallas import tpu as pltpu
from jax.sharding import PartitionSpec as P

MESH = pl.DeviceIdType.MESH
TS = 16
SLOTS = 6
LANES = 128
UNITS = 8
AXES = ((0, 1, 2), (1, 2, 0), (2, 0, 1))
GROUP = SLOTS * 4
BLOCK = 4 * GROUP
F32 = jnp.float32
BF16 = jnp.bfloat16


def split2(a):
    hi = a.astype(BF16)
    return hi, (a - hi.astype(F32)).astype(BF16)


def dot(a, b, dims=((1,), (0,))):
    return lax.dot_general(a, b, (dims, ((), ())), preferred_element_type=F32)


def dot3(a, b, dims=((1,), (0,))):
    ah, al = a
    bh, bl = b
    return dot(ah, bh, dims) + (dot(ah, bl, dims) + dot(al, bh, dims))


def dot_f32(a, b, dims=((1,), (0,))):
    return lax.dot_general(
        a, b, (dims, ((), ())), precision=lax.Precision.HIGHEST, preferred_element_type=F32
    )


def iota(shape, axis):
    return lax.broadcasted_iota(jnp.int32, shape, axis)


def block_transpose(vectors):
    lane_block = iota((8, LANES), 1) // TS
    vectors = list(vectors)
    for bit in (4, 2, 1):
        low = (lane_block & bit) == 0
        result = [None] * 8
        for a in range(8):
            if a & bit:
                continue
            b = a | bit
            up, down = vectors[a], vectors[b]
            result[a] = jnp.where(low, up, pltpu.roll(down, bit * TS, 1))
            result[b] = jnp.where(low, pltpu.roll(up, LANES - bit * TS, 1), down)
        vectors = result
    return vectors


def powers(logs, exponent):
    return jnp.exp(exponent.astype(F32) * logs)


def whole(ref, first, count, sem):
    part = ref.at[pl.ds(first, count)]
    pltpu.make_async_copy(part, part, sem).wait()


def kernel(
    source_ref, target_ref, potential_ref, device_ref, tile_ref, count_ref, reach_hbm,
    pushed_ref, next_ref,
    natural, target, potential, gathered, smooth, reach_ref,
    meta, metas, tiles, spread_in, picks, weights, places,
    slots_out, slots_in, labels_out, labels_in, partial_out, partial_in, own_sum,
    xtab_hi, xtab_lo, ytab_hi, ytab_lo, xmsg, xall, ymsg, yall,
    load_sem, store_sem, meta_send, meta_recv, spread_send, spread_recv,
    slot_send, slot_recv, label_send, label_recv, partial_send, partial_recv,
    x_send, x_recv, y_send, y_recv,
):
    p, q = lax.axis_index("gx"), lax.axis_index("gy")
    n_gx, n_gy = 8, 16
    planes, cx, cy = source_ref.shape
    tile_rows, tile_cols = cx // TS, cy // TS
    here = (q & 3, p >> 1, q >> 2)
    core = p & 1
    stride = (1, 2 * n_gy, 4)

    def device(moves, other):
        x, y, z = [(here[axis] + moves.get(axis, 0)) & 3 for axis in range(3)]
        return y * 2 + (core ^ other), z * 4 + x

    def remote(src, dst, send, recv, to):
        pltpu.make_async_remote_copy(
            src_ref=src, dst_ref=dst, send_sem=send, recv_sem=recv,
            device_id=to, device_id_type=MESH,
        ).start()

    loads = [
        pltpu.make_async_copy(a, b, load_sem.at[i])
        for i, (a, b) in enumerate([
            (device_ref, meta.at[0]), (tile_ref, meta.at[1]), (count_ref, meta.at[2]),
            (source_ref, natural), (target_ref, target), (potential_ref, potential),
            (reach_hbm, reach_ref),
        ])
    ]
    for load in loads:
        load.start()

    barrier = pltpu.get_barrier_semaphore()
    peers = [({axis: s}, h) for axis in range(3) for s in range(1, 4) for h in range(2)]
    peers.append(({}, 1))
    for moves, other in peers:
        pl.semaphore_signal(
            barrier, inc=1, device_id=device(moves, other), device_id_type=MESH
        )

    for load in loads[:4]:
        load.wait()
    for xo in range(tile_rows):
        parts = [
            natural[g // 2, pl.ds(xo * TS + (g % 2) * 8, 8), :] for g in range(2 * planes)
        ]
        for yo, value in enumerate(block_transpose(parts)):
            tiles[pl.ds(xo * tile_cols + yo, UNITS, stride=LANES), :] = value
    pl.semaphore_wait(barrier, len(peers))

    for g, (a, _, _) in enumerate(AXES):
        for s in range(1, 4):
            remote(meta, metas.at[g * 3 + s - 1], meta_send, meta_recv.at[g], device({a: s}, 0))
    for c in range(UNITS):
        for s in range(1, 4):
            remote(
                tiles.at[pl.ds(c * LANES, LANES)],
                spread_in.at[pl.ds((c * 3 + s - 1) * LANES, LANES)],
                spread_send, spread_recv.at[c], device({AXES[c % 3][0]: s}, 0),
            )

    earlier = (iota((LANES, LANES), 0) < iota((LANES, LANES), 1)).astype(BF16)
    row = iota((GROUP, LANES), 0)
    row_k, row_j = (row >> 2).astype(F32), row & 3

    def find_slots(g, s, info):
        a, b, e = AXES[g]
        names, spots, counts = info[0], info[1].astype(F32), info[2].astype(F32)
        shares = counts / jnp.sum(counts, axis=0, keepdims=True)
        along = ((here[e] + row_j) & 3) * stride[e]
        masks = []
        for ih in range(8):
            number = (
                here[a] * stride[a] + ((here[b] + ih // 2) & 3) * stride[b]
                + (core ^ (ih % 2)) * n_gy + along
            )
            share = jnp.zeros((GROUP, LANES), F32)
            spot = jnp.zeros((GROUP, LANES), F32)
            for f in range(4):
                match = number == names[f : f + 1, :]
                share = jnp.where(match, shares[f : f + 1, :], share)
                spot = jnp.where(match, spots[f : f + 1, :], spot)
            masks.append((share, spot))
        share = jnp.concatenate([m[0] for m in masks], axis=0)
        named = jnp.where(share > 0.0, 1.0, 0.0)
        rank = dot(named.astype(BF16), earlier)
        wanted = jnp.concatenate([row_k] * 8, axis=0)
        pick = jnp.where(rank == wanted, named, 0.0)
        picks[g * 4 + s] = pick.astype(BF16)
        weights[g * 4 + s] = jnp.broadcast_to(
            jnp.sum(pick * share, axis=1, keepdims=True), (8 * GROUP, LANES)
        )
        for ih in range(8):
            places[g, pl.ds(ih * LANES + s * GROUP, GROUP), :] = (
                pick[ih * GROUP : (ih + 1) * GROUP] * masks[ih][1]
            )

    for g, (a, b, _) in enumerate(AXES):
        whole(metas, g * 3, 3, meta_recv.at[g])
        for s in range(4):
            find_slots(g, s, meta[...] if s == 0 else metas[g * 3 + s - 1])
        for ih in range(8):
            places[g, pl.ds(ih * LANES + BLOCK, LANES - BLOCK), :] = jnp.zeros(
                (LANES - BLOCK, LANES), F32
            )
        found = dot(jnp.ones((8, LANES), BF16), places[g].astype(BF16), ((1,), (1,)))
        for ih in range(8):
            line = found[0:1, ih * LANES : (ih + 1) * LANES]
            if ih == 0:
                labels_in[g * 8] = line
            else:
                labels_out[g * 8 + ih] = line
        for ih in range(1, 8):
            remote(
                labels_out.at[g * 8 + ih], labels_in.at[g * 8 + ih],
                label_send, label_recv.at[g], device({b: ih // 2}, ih % 2),
            )

    for c in range(UNITS):
        g = c % 3
        b = AXES[g][1]
        for s in range(4):
            if s == 1:
                whole(spread_in, c * 3 * LANES, 3 * LANES, spread_recv.at[c])
            if s == 0:
                value = tiles[pl.ds(c * LANES, LANES), :]
            else:
                value = spread_in[pl.ds((c * 3 + s - 1) * LANES, LANES), :]
            pick = picks[g * 4 + s]
            value = dot(
                jnp.concatenate([pick, pick], axis=1), jnp.concatenate(split2(value), axis=0)
            )
            value = value * weights[g * 4 + s]
            for ih in range(8):
                piece = value[ih * GROUP : (ih + 1) * GROUP]
                if ih == 0:
                    slots_in[pl.ds(c * 8 * BLOCK + s * GROUP, GROUP), :] = piece
                else:
                    slots_out[pl.ds((c * 7 + ih - 1) * BLOCK + s * GROUP, GROUP), :] = piece
        for ih in range(1, 8):
            remote(
                slots_out.at[pl.ds((c * 7 + ih - 1) * BLOCK, BLOCK)],
                slots_in.at[pl.ds((c * 8 + ih) * BLOCK, BLOCK)],
                slot_send, slot_recv.at[c], device({b: ih // 2}, ih % 2),
            )

    loads[6].wait()
    decay = [jnp.full((1, 1), 1.0 - 1.0 / reach_ref[z], F32) for z in range(planes)]
    logs = [jnp.log(d) for d in decay]
    scale = [(1.0 - d) ** 2 for d in decay]

    def tables(z, n):
        at = iota((1, n), 1)
        gap = iota((n, n), 0) - iota((n, n), 1)
        lower = jnp.where(gap >= 0, powers(logs[z], jnp.maximum(gap, 0)), 0.0)
        both = scale[z] * dot_f32(lower, lower, ((0,), (0,)))
        last = powers(logs[z], n - 1 - at)
        rise = powers(logs[z], at + 1)
        fall = powers(logs[z], n - at)
        swept = scale[z] * dot_f32(jnp.broadcast_to(rise, (8, n)), lower)[0:1]
        return both, (last, swept, fall, both[0:1])

    x_edges, y_edges = [], []
    for z in range(planes):
        both, edge = tables(z, cx)
        xtab_hi[z], xtab_lo[z] = split2(both)
        x_edges.append(edge)
        both, edge = tables(z, cy)
        ytab_hi[z], ytab_lo[z] = split2(both)
        y_edges.append(edge)

    wide = 8 * SLOTS * 4
    out_lane = iota((1, wide), 1)
    sender = jnp.zeros((1, wide), jnp.int32)
    for m in range(1, 8):
        sender += (out_lane >= m * GROUP).astype(jnp.int32)
    within = out_lane - sender * GROUP
    in_lane = iota((LANES, wide), 0)
    sender_row = iota((8, wide), 0) == sender
    tile_index = iota((LANES, wide), 0).astype(F32)
    selects = []
    for g in range(3):
        whole(labels_in, g * 8 + 1, 7, label_recv.at[g])
        lines = labels_in[pl.ds(g * 8, 8)].reshape(8, LANES).astype(BF16)
        row_of = []
        for j in range(4):
            choose = ((in_lane >> 2) == within) & ((in_lane & 3) == j)
            named = dot(lines, choose.astype(BF16))
            named = jnp.sum(jnp.where(sender_row, named, 0.0), axis=0, keepdims=True)
            row_of.append((tile_index == named).astype(BF16))
        selects.append(row_of)

    for c in range(UNITS):
        g = c % 3
        whole(slots_in, (c * 8 + 1) * BLOCK, 7 * BLOCK, slot_recv.at[c])
        for j in range(4):
            rows = slots_in[pl.ds(c * 8 * BLOCK + j, wide, stride=4), :]
            value = dot(selects[g][j], jnp.concatenate(split2(rows), axis=1))
            value = value[:, :LANES] + value[:, LANES:]
            if j == 0:
                own_sum[pl.ds(c * LANES, LANES), :] = value
            else:
                at = pl.ds((c * 3 + j - 1) * LANES, LANES)
                partial_out[at, :] = value
                remote(
                    partial_out.at[at], partial_in.at[at],
                    partial_send, partial_recv.at[c], device({AXES[g][2]: j}, 0),
                )

    for c in range(UNITS):
        whole(partial_in, c * 3 * LANES, 3 * LANES, partial_recv.at[c])
        at = pl.ds(c * LANES, LANES)
        total = own_sum[at, :]
        for j in range(3):
            total += partial_in[pl.ds((c * 3 + j) * LANES, LANES), :]
        own_sum[at, :] = total
    for xo in range(tile_rows):
        parts = [
            own_sum[pl.ds(xo * tile_cols + yo, UNITS, stride=LANES), :]
            for yo in range(tile_cols)
        ]
        for g, value in enumerate(block_transpose(parts)):
            gathered[g // 2, pl.ds(xo * TS + (g % 2) * 8, 8), :] = value
    store_pushed = pltpu.make_async_copy(gathered, pushed_ref, store_sem.at[0])
    store_pushed.start()

    loads[4].wait()
    row8 = iota((8, 1), 0)
    ends = jnp.zeros((8, cy), F32)
    for z in range(planes):
        mismatch = target[z] - gathered[z]
        base = dot3((xtab_hi[z], xtab_lo[z]), split2(mismatch))
        smooth[z] = base
        ends += dot_f32(jnp.where(row8 == z, x_edges[z][0], 0.0), mismatch)
        ends += jnp.where(row8 == planes + z, base[0:1], 0.0)
    xmsg[...] = ends
    for s in range(4):
        for h in range(2):
            if s + h:
                remote(xmsg, xall.at[p], x_send, x_recv, device({1: s}, h))
    xall[p] = ends
    whole(xall, 0, n_gx - 1, x_recv)

    def boundary(all_ref, count, at, across, first_swept, width):
        low = row8 < planes
        entering = jnp.zeros((8, width), F32)
        entry, picked = [], jnp.zeros((8, width), F32)
        for i in range(count):
            entry.append(entering)
            picked = jnp.where(at == i, entering, picked)
            entering = jnp.where(low, across * entering + all_ref[i], 0.0)
        leaving = jnp.zeros((8, width), F32)
        out = jnp.zeros((8, width), F32)
        for i in reversed(range(count)):
            out = jnp.where(at == i, leaving, out)
            begun = all_ref[i] + pltpu.roll(first_swept * entry[i], planes, 0)
            leaving = jnp.where(low, 0.0, across * leaving + begun)
        return picked + out

    def column8(values):
        result = jnp.zeros((8, 1), F32)
        for z, v in enumerate(values):
            result = jnp.where((row8 == z) | (row8 == planes + z), v, result)
        return result

    across_x = column8([powers(logs[z], jnp.full((1, 1), cx, jnp.int32)) for z in range(planes)])
    across_y = column8([powers(logs[z], jnp.full((1, 1), cy, jnp.int32)) for z in range(planes)])
    swept_x = column8([x_edges[z][1][:, 0:1] for z in range(planes)])
    swept_y = column8([y_edges[z][1][:, 0:1] for z in range(planes)])

    def spread(z, edge):
        return jnp.where(row8 == z, edge[1], 0.0) + jnp.where(row8 == planes + z, edge[2], 0.0)

    inflow = boundary(xall, n_gx, p, across_x, swept_x, cy)
    ends = jnp.zeros((8, cx), F32)
    for z in range(planes):
        value = smooth[z] + dot_f32(spread(z, x_edges[z]), inflow, ((0,), (0,)))
        smooth[z] = value
        weights8 = jnp.where(row8 == z, y_edges[z][0], 0.0) + jnp.where(
            row8 == planes + z, y_edges[z][3], 0.0
        )
        ends += dot_f32(weights8, value, ((1,), (1,)))
    ymsg[...] = ends
    for dz in range(4):
        for dx in range(4):
            if dz + dx:
                remote(ymsg, yall.at[q], y_send, y_recv, device({2: dz, 0: dx}, 0))
    yall[q] = ends
    loads[5].wait()
    for z in range(planes):
        potential[z] = potential[z] + dot3(split2(smooth[z]), (ytab_hi[z], ytab_lo[z]))
    whole(yall, 0, n_gy - 1, y_recv)
    inflow = boundary(yall, n_gy, q, across_y, swept_y, cx)
    for z in range(planes):
        potential[z] = potential[z] + dot_f32(inflow, spread(z, y_edges[z]), ((0,), (0,)))
    store_next = pltpu.make_async_copy(potential, next_ref, store_sem.at[1])
    store_next.start()

    whole(metas, 0, 9, meta_send)
    whole(spread_in, 0, 3 * UNITS * LANES, spread_send)
    whole(slots_out, 0, 7 * UNITS * BLOCK, slot_send)
    whole(labels_out, 0, 21, label_send)
    whole(partial_out, 0, 3 * UNITS * LANES, partial_send)
    whole(xall, 0, n_gx - 1, x_send)
    whole(yall, 0, n_gy - 1, y_send)
    store_pushed.wait()
    store_next.wait()


def per_device(source_mass, target_density, potential, dest_device, dest_tile, mass_counts, reach):
    planes, cx, cy = source_mass.shape

    def lanes(a):
        return jnp.swapaxes(a.reshape(a.shape[2:]), 0, 1)

    hbm = pl.BlockSpec(memory_space=pl.ANY)
    dma = pltpu.SemaphoreType.DMA
    vmem = pltpu.VMEM
    grid = jax.ShapeDtypeStruct((planes, cx, cy), F32)
    field = vmem((planes, cx, cy), F32)
    return pl.pallas_call(
        kernel,
        out_shape=(grid, grid),
        in_specs=[hbm] * 7,
        out_specs=(hbm, hbm),
        scratch_shapes=[
            field, field, field, field, field,
            pltpu.SMEM((planes,), F32),
            vmem((3, 4, LANES), jnp.int32),
            vmem((9, 3, 4, LANES), jnp.int32),
            vmem((UNITS * LANES, LANES), F32),
            vmem((3 * UNITS * LANES, LANES), F32),
            vmem((12, 8 * GROUP, LANES), BF16),
            vmem((12, 8 * GROUP, LANES), F32),
            vmem((3, 8 * LANES, LANES), F32),
            vmem((7 * UNITS * BLOCK, LANES), F32),
            vmem((8 * UNITS * BLOCK, LANES), F32),
            vmem((24, 1, LANES), F32),
            vmem((24, 1, LANES), F32),
            vmem((3 * UNITS * LANES, LANES), F32),
            vmem((3 * UNITS * LANES, LANES), F32),
            vmem((UNITS * LANES, LANES), F32),
            vmem((planes, cx, cx), BF16),
            vmem((planes, cx, cx), BF16),
            vmem((planes, cy, cy), BF16),
            vmem((planes, cy, cy), BF16),
            vmem((8, cy), F32),
            vmem((8, 8, cy), F32),
            vmem((8, cx), F32),
            vmem((16, 8, cx), F32),
            dma((7,)), dma((2,)), dma, dma((3,)), dma, dma((UNITS,)),
            dma, dma((UNITS,)), dma, dma((3,)), dma, dma((UNITS,)),
            dma, dma, dma, dma,
        ],
        compiler_params=pltpu.CompilerParams(collective_id=0, has_side_effects=True),
        name="dual_step",
    )(
        source_mass, target_density, potential,
        lanes(dest_device), lanes(dest_tile), lanes(mass_counts), reach,
    )


def solution(mesh):
    in_specs = (
        P(None, "gx", "gy"),
        P(None, "gx", "gy"),
        P(None, "gx", "gy"),
        P("gx", "gy", None, None),
        P("gx", "gy", None, None),
        P("gx", "gy", None, None),
        P(),
    )
    out_specs = (P(None, "gx", "gy"), P(None, "gx", "gy"))
    return jax.shard_map(
        per_device, mesh=mesh, in_specs=in_specs, out_specs=out_specs, check_vma=False
    )
```

time: 73.5 us -> 55.3 us (0.75)
  Pallas kernels: 66.5 us -> 51.8 us
  local copies, waits for them, and re-layouts: 6.07 us -> 2.72 us
    pallas_call x1, Pallas kernels: 66.5 us -> 51.8 us  [per_device(): pl.pallas_call(kernel, out_shape=(grid, grid), in_specs=[hbm] * 7, out_sp...]
    unnamed x16 -> x4, local copies, waits for them, and re-layouts: 6.07 us -> 2.72 us
where the time goes in v2:
time: 55.3 us; the launch traced here: 55.2 us
  Pallas kernels  51.8 us (94%)
  local copies, waits for them, and re-layouts  2.72 us (5%)
  between operations  0.65 us (1%)
    pallas_call x1, Pallas kernels, per_device(): pl.pallas_call(kernel, out_shape=(grid, grid), in_specs=[hbm] * 7, out_sp...  51.8 us
    unnamed x4, local copies, waits for them, and re-layouts  2.72 us

profile of v2, /device:TPU:0, one launch (start us, length us, event | category | flops | bytes accessed | tf_op | source)
XLA Modules:
  0.0 55.2 jit_solution(8600157878939970220)
XLA Ops:
  0.6 51.8 %dual_step.1 = (f32[4,256,128]{2,1,0:T(8,128)}, f32[4,256,128]{2,1,0:T(8,128)}) custom-call(f32[4,256,128]{2,1,0:T(8,128)} %source_ref.1, f32[4,256,128]{2,1,0:T(8,128)} %target_ref.1, f32[4,256,128]{2,1,0:T(8,128)} %potential_ref.1, s32[4,128]{1,0:T(4,128)} %bitcast.9, s32[4,128]{1,0:T(4,128)} %bitcast.10, s32[4,128]{1,0:T(4,128)} %bitcast.11, f32[4]{0:T(128)} %reach_hbm.1), custom_call_target="tpu_custom_call" | custom-call | tf_op jit(solution)/shard_map/dual_step/pallas_call | solution.py:399
  52.4 0.0 copy-start
  52.4 1.9 %copy.11 = f32[4,256,128]{2,1,0:T(8,128)} copy(f32[4,256,128]{2,1,0:T(8,128)} %get-tuple-element.4) | data formatting | bytes 1048576
  54.4 0.0 copy-done
  54.4 0.8 %copy.12 = f32[4,256,128]{2,1,0:T(8,128)} copy(f32[4,256,128]{2,1,0:T(8,128)S(1)} %copy-done) | data formatting | bytes 1048576
Async XLA Ops:
  52.4 1.9 %copy-start = (f32[4,256,128]{2,1,0:T(8,128)S(1)}, f32[4,256,128]{2,1,0:T(8,128)}, u32[]{:S(2)}) copy-start(f32[4,256,128]{2,1,0:T(8,128)} %get-tuple-element.5) | copy-start | bytes 1572868

commit v3 on v2

v3 whole, which is shorter than its diff:
```python
import jax
import jax.numpy as jnp
from jax import lax
from jax.experimental import pallas as pl
from jax.experimental.pallas import tpu as pltpu
from jax.sharding import PartitionSpec as P

MESH = pl.DeviceIdType.MESH
TS = 16
SLOTS = 6
LANES = 128
UNITS = 8
AXES = ((0, 1, 2), (1, 2, 0), (2, 0, 1))
GROUP = SLOTS * 4
BLOCK = 4 * GROUP
PITCH = 9
F32 = jnp.float32
BF16 = jnp.bfloat16


def split2(a):
    hi = a.astype(BF16)
    return hi, (a - hi.astype(F32)).astype(BF16)


def dot(a, b, dims=((1,), (0,))):
    return lax.dot_general(a, b, (dims, ((), ())), preferred_element_type=F32)


def dot3(a, b, dims=((1,), (0,))):
    ah, al = a
    bh, bl = b
    return dot(ah, bh, dims) + (dot(ah, bl, dims) + dot(al, bh, dims))


def dot_f32(a, b, dims=((1,), (0,))):
    return lax.dot_general(
        a, b, (dims, ((), ())), precision=lax.Precision.HIGHEST, preferred_element_type=F32
    )


def iota(shape, axis):
    return lax.broadcasted_iota(jnp.int32, shape, axis)


def block_transpose(vectors):
    lane_block = iota((8, LANES), 1) // TS
    vectors = list(vectors)
    for bit in (4, 2, 1):
        low = (lane_block & bit) == 0
        result = [None] * 8
        for a in range(8):
            if a & bit:
                continue
            b = a | bit
            up, down = vectors[a], vectors[b]
            result[a] = jnp.where(low, up, pltpu.roll(down, bit * TS, 1))
            result[b] = jnp.where(low, pltpu.roll(up, LANES - bit * TS, 1), down)
        vectors = result
    return vectors


def powers(logs, exponent):
    return jnp.exp(exponent.astype(F32) * logs)


def whole(ref, first, count, sem):
    part = ref.at[pl.ds(first, count)]
    pltpu.make_async_copy(part, part, sem).wait()


def kernel(
    source_ref, target_ref, potential_ref, device_ref, tile_ref, count_ref, reach_hbm,
    pushed_ref, next_ref,
    natural, target, potential, smooth, reach_ref,
    meta, metas, tiles, regroup, spread_in, picks, weights, places,
    slots_out, slots_in, labels_out, labels_in,
    far_out, far_in, partial_out, partial_in, own_sum,
    xtab_hi, xtab_lo, ytab_hi, ytab_lo, xends_tab, yends_tab, xfill, yfill_tab,
    coef, edge_rows, halves, xmsg, xall, ymsg, yall,
    load_sem, meta_send, meta_recv, spread_send, spread_recv, relay_recv,
    slot_send, slot_recv, label_send, label_recv, far_send, far_recv,
    partial_send, partial_recv, x_send, x_recv, y_send, y_recv,
):
    p, q = lax.axis_index("gx"), lax.axis_index("gy")
    n_gx, n_gy = 8, 16
    planes, cx, cy = source_ref.shape
    tile_rows, tile_cols = cx // TS, cy // TS
    half = LANES // 2
    here = (q & 3, p >> 1, q >> 2)
    core = p & 1
    stride = (1, 2 * n_gy, 4)

    def device(moves, other):
        x, y, z = [(here[axis] + moves.get(axis, 0)) & 3 for axis in range(3)]
        return y * 2 + (core ^ other), z * 4 + x

    def remote(src, dst, send, recv, to):
        pltpu.make_async_remote_copy(
            src_ref=src, dst_ref=dst, send_sem=send, recv_sem=recv,
            device_id=to, device_id_type=MESH,
        ).start()

    loads = [
        pltpu.make_async_copy(a, b, load_sem.at[i])
        for i, (a, b) in enumerate([
            (device_ref, meta.at[0]), (tile_ref, meta.at[1]), (count_ref, meta.at[2]),
            (source_ref, natural), (target_ref, target), (potential_ref, potential),
            (reach_hbm, reach_ref),
        ])
    ]
    for load in loads:
        load.start()

    barrier = pltpu.get_barrier_semaphore()
    peers = [({axis: s}, h) for axis in range(3) for s in range(1, 4) for h in range(2)]
    peers.append(({}, 1))
    for moves, other in peers:
        pl.semaphore_signal(
            barrier, inc=1, device_id=device(moves, other), device_id_type=MESH
        )

    for load in loads[:4]:
        load.wait()
    for xo in range(tile_rows):
        parts = [
            natural[g // 2, pl.ds(xo * TS + (g % 2) * 8, 8), :] for g in range(2 * planes)
        ]
        for yo, value in enumerate(block_transpose(parts)):
            regroup[pl.ds((xo * tile_cols + yo) * PITCH, UNITS), :] = value
    for c in range(UNITS):
        tiles[pl.ds(c * LANES, LANES), :] = regroup[pl.ds(c, LANES, stride=PITCH), :]
    pl.semaphore_wait(barrier, len(peers))

    def spread_row(c, s):
        return (c * 3 + s) * LANES

    for g, (a, _, _) in enumerate(AXES):
        for s in range(1, 4):
            remote(meta, metas.at[g * 3 + s - 1], meta_send, meta_recv.at[g], device({a: s}, 0))
    for c in range(UNITS):
        for s, move in enumerate((1, 3)):
            remote(
                tiles.at[pl.ds(c * LANES, LANES)],
                spread_in.at[pl.ds(spread_row(c, s), LANES)],
                spread_send, spread_recv.at[c], device({AXES[c % 3][0]: move}, 0),
            )

    def relay_tiles(c):
        whole(spread_in, spread_row(c, 0), 2 * LANES, spread_recv.at[c])
        for s, move in enumerate((1, 3)):
            remote(
                spread_in.at[pl.ds(spread_row(c, s) + s * half, half)],
                spread_in.at[pl.ds(spread_row(c, 2) + s * half, half)],
                spread_send, relay_recv.at[c], device({AXES[c % 3][0]: move}, 0),
            )

    earlier = (iota((LANES, LANES), 0) < iota((LANES, LANES), 1)).astype(BF16)
    row = iota((32, LANES), 0)
    row_target, row_j = row >> 2, row & 3
    order = iota((8, LANES), 0).astype(F32)

    def find_slots(g, s, info):
        a, b, e = AXES[g]
        names, spots, counts = info[0], info[1].astype(F32), info[2].astype(F32)
        shares = counts / jnp.sum(counts, axis=0, keepdims=True)
        number = (
            here[a] * stride[a] + ((here[b] + (row_target >> 1)) & 3) * stride[b]
            + (core ^ (row_target & 1)) * n_gy + ((here[e] + row_j) & 3) * stride[e]
        )
        share = jnp.zeros((32, LANES), F32)
        spot = jnp.zeros((32, LANES), F32)
        for f in range(4):
            match = number == names[f : f + 1, :]
            share = jnp.where(match, shares[f : f + 1, :], share)
            spot = jnp.where(match, spots[f : f + 1, :], spot)
        named = share > 0.0
        rank = dot(jnp.where(named, 1.0, 0.0).astype(BF16), earlier)
        rank = jnp.where(named, rank, -1.0)
        found = []
        for r in range(32):
            mine = rank[r : r + 1, :] == order
            found.append(jnp.where(mine, 1.0, 0.0))
            part = jnp.where(mine, share[r : r + 1, :], 0.0)
            weights[g * 4 + s, pl.ds(r * 8, 8), :] = jnp.broadcast_to(
                jnp.sum(part, axis=1, keepdims=True), (8, LANES)
            )
            places[g, pl.ds((r // 4) * LANES + (r % 4) * GROUP + s * SLOTS, SLOTS), :] = (
                jnp.where(mine, spot[r : r + 1, :], 0.0)[:SLOTS]
            )
        picks[g * 4 + s] = jnp.concatenate(found, axis=0).astype(BF16)

    source_meta = (None, 0, 2, 1)

    def find_labels(g):
        b = AXES[g][1]
        for ih in range(8):
            places[g, pl.ds(ih * LANES + BLOCK, LANES - BLOCK), :] = jnp.zeros(
                (LANES - BLOCK, LANES), F32
            )
        found = dot(jnp.ones((8, LANES), BF16), places[g].astype(BF16), ((1,), (1,)))
        for ih in range(8):
            line = found[0:1, ih * LANES : (ih + 1) * LANES]
            if ih == 0:
                labels_in[g * 8] = line
            else:
                labels_out[g * 8 + ih - 1] = line
        for ih in range(1, 8):
            remote(
                labels_out.at[g * 8 + ih - 1], labels_in.at[g * 8 + ih],
                label_send, label_recv.at[g], device({b: ih // 2}, ih % 2),
            )

    for g in range(3):
        find_slots(g, 0, meta[...])
    for g in range(3):
        whole(metas, g * 3, 3, meta_recv.at[g])
        for s in range(1, 4):
            find_slots(g, s, metas[g * 3 + source_meta[s]])
        for c in range(g, UNITS, 3)[:1]:
            relay_tiles(c)
    for g in range(3):
        find_labels(g)
    for c in range(3, UNITS):
        relay_tiles(c)

    def pack(c):
        g = c % 3
        b = AXES[g][1]
        for s in range(4):
            if s == 3:
                whole(spread_in, spread_row(c, 2), LANES, relay_recv.at[c])
            if s == 0:
                value = tiles[pl.ds(c * LANES, LANES), :]
            else:
                value = spread_in[pl.ds(spread_row(c, s - 1), LANES), :]
            pick = picks[g * 4 + s]
            value = dot(
                jnp.concatenate([pick, pick], axis=1), jnp.concatenate(split2(value), axis=0)
            )
            value = value * weights[g * 4 + s]
            for r in range(32):
                ih, j = r // 4, r % 4
                piece = value[r * 8 : r * 8 + SLOTS]
                within = j * GROUP + s * SLOTS
                if ih == 0:
                    slots_in[pl.ds(c * 8 * BLOCK + within, SLOTS), :] = piece
                else:
                    slots_out[pl.ds((c * 7 + ih - 1) * BLOCK + within, SLOTS), :] = piece
        for ih in range(1, 8):
            remote(
                slots_out.at[pl.ds((c * 7 + ih - 1) * BLOCK, BLOCK)],
                slots_in.at[pl.ds((c * 8 + ih) * BLOCK, BLOCK)],
                slot_send, slot_recv.at[c], device({b: ih // 2}, ih % 2),
            )

    for c in range(UNITS):
        pack(c)

    loads[6].wait()
    decay = [jnp.full((1, 1), 1.0 - 1.0 / reach_ref[z], F32) for z in range(planes)]
    logs = [jnp.log(d) for d in decay]
    scale = [(1.0 - d) ** 2 for d in decay]
    row8 = iota((8, 1), 0)

    def both_rows(values):
        result = jnp.zeros((8, values[0].shape[1]), F32)
        for z, v in enumerate(values):
            result = jnp.where((row8 == z) | (row8 == planes + z), v, result)
        return result

    def stacked(a):
        hi = a.astype(BF16).astype(F32)
        return jnp.concatenate([hi, a - hi], axis=0).astype(BF16)

    swept_first, last_rows, first_rows = {}, {}, {}
    for axis, n in (("x", cx), ("y", cy)):
        at = iota((1, n), 1)
        gap = iota((n, n), 0) - iota((n, n), 1)
        lasts, firsts, swepts, falls = [], [], [], []
        for z in range(planes):
            lower = jnp.where(gap >= 0, powers(logs[z], jnp.maximum(gap, 0)), 0.0)
            both = scale[z] * dot_f32(lower, lower, ((0,), (0,)))
            last = powers(logs[z], n - 1 - at)
            rise = powers(logs[z], at + 1)
            fall = powers(logs[z], n - at)
            swept = scale[z] * dot_f32(jnp.broadcast_to(rise, (8, n)), lower)[0:1]
            lasts.append(last)
            firsts.append(both[0:1])
            swepts.append(swept)
            falls.append(fall)
            ends = jnp.where(row8 == z, last, 0.0) + jnp.where(
                row8 == planes + z, both[0:1], 0.0
            )
            if axis == "x":
                xtab_hi[z], xtab_lo[z] = split2(both)
                xends_tab[z] = stacked(ends)
                down = iota((n, LANES), 0)
                xfill[z] = scale[z] * dot_f32(lower, powers(logs[z], down + 1), ((0,), (0,)))
                xfill[planes + z] = powers(logs[z], n - down)
            else:
                ytab_hi[z], ytab_lo[z] = split2(both)
                yends_tab[z] = stacked(ends)
                fill = jnp.where(row8 == z, swept, 0.0) + jnp.where(
                    row8 == planes + z, fall, 0.0
                )
                hi = fill.astype(BF16).astype(F32)
                yfill_tab[z] = jnp.concatenate([hi, hi, fill - hi, fill - hi], axis=0).astype(
                    BF16
                )
        swept_first[axis] = both_rows([v[:, 0:1] for v in swepts])
        if axis == "x":
            edge_rows[0] = both_rows(swepts)
            edge_rows[1] = both_rows(falls)
        else:
            last_rows, first_rows = both_rows(lasts), both_rows(firsts)

    def coefficients(base, count, at, n, first):
        across = both_rows([powers(logs[z], jnp.full((1, 1), n, jnp.int32)) for z in range(planes)])
        powers_of = [jnp.ones((8, 1), F32)]
        for _ in range(count - 1):
            powers_of.append(powers_of[-1] * across)
        low = row8 < planes
        before, after = [], []
        for i in range(count):
            coming = jnp.zeros((8, 1), F32)
            going = jnp.zeros((8, 1), F32)
            for m in range(count - 1):
                coming = jnp.where(at - 1 - i == m, powers_of[m], coming)
                going = jnp.where(i - at - 1 == m, powers_of[m], going)
            before.append(coming)
            after.append(going)
        through = jnp.zeros((8, 1), F32)
        crossing = [None] * count
        for i in reversed(range(count)):
            crossing[i] = first * through
            through = after[i] + across * through
        for i in range(count):
            coef[base + i] = jnp.broadcast_to(jnp.where(low, before[i], after[i]), (8, LANES))
            coef[base + count + i] = jnp.broadcast_to(
                jnp.where(low, crossing[i], 0.0), (8, LANES)
            )

    coefficients(0, n_gx, p, cx, swept_first["x"])
    coefficients(2 * n_gx, n_gy, q, cy, swept_first["y"])

    def inflow(base, count, all_ref, width):
        columns = []
        for w in range(width // LANES):
            direct, through = [], []
            for i in range(count):
                value = all_ref[i, :, pl.ds(w * LANES, LANES)]
                direct.append(coef[base + i] * value)
                through.append(coef[base + count + i] * value)
            while len(direct) > 1:
                direct = [a + b for a, b in zip(direct[::2], direct[1::2])]
                through = [a + b for a, b in zip(through[::2], through[1::2])]
            columns.append(direct[0] + pltpu.roll(through[0], planes, 0))
        return columns[0] if len(columns) == 1 else jnp.concatenate(columns, axis=1)

    wide = 8 * GROUP
    out_lane = iota((1, wide), 1)
    sender = jnp.zeros((1, wide), jnp.int32)
    for m in range(1, 8):
        sender += (out_lane >= m * GROUP).astype(jnp.int32)
    within = out_lane - sender * GROUP
    in_lane = iota((LANES, wide), 0)
    sender_row = iota((8, wide), 0) == sender
    tile_index = iota((LANES, wide), 0).astype(F32)
    selects = []
    for g in range(3):
        whole(labels_in, g * 8 + 1, 7, label_recv.at[g])
        lines = labels_in[pl.ds(g * 8, 8)].reshape(8, LANES).astype(BF16)
        row_of = []
        for j in range(4):
            choose = in_lane == within + j * GROUP
            named = dot(lines, choose.astype(BF16))
            named = jnp.sum(jnp.where(sender_row, named, 0.0), axis=0, keepdims=True)
            row_of.append((tile_index == named).astype(BF16))
        selects.append(row_of)

    def partial_row(c, s):
        return (c * 2 + s) * LANES

    def unpack(c):
        g = c % 3
        e = AXES[g][2]
        whole(slots_in, (c * 8 + 1) * BLOCK, 7 * BLOCK, slot_recv.at[c])
        for j in (2, 1, 3, 0):
            rows = jnp.concatenate(
                [
                    slots_in[pl.ds((c * 8 + ih) * BLOCK + j * GROUP, GROUP), :]
                    for ih in range(8)
                ],
                axis=0,
            )
            value = dot(selects[g][j], jnp.concatenate(split2(rows), axis=1))
            value = value[:, :LANES] + value[:, LANES:]
            if j == 0:
                own_sum[pl.ds(c * LANES, LANES), :] = value
            elif j == 2:
                far_out[pl.ds(c * LANES, LANES), :] = value
                for s, move in enumerate((1, 3)):
                    remote(
                        far_out.at[pl.ds(c * LANES + s * half, half)],
                        far_in.at[pl.ds(c * LANES + s * half, half)],
                        far_send, far_recv.at[c], device({e: move}, 0),
                    )
            else:
                s, move = (0, 1) if j == 1 else (1, 3)
                partial_out[pl.ds(partial_row(c, s), LANES), :] = value
                at = pl.ds(partial_row(c, s) + (1 - s) * half, half)
                remote(
                    partial_out.at[at], partial_in.at[at],
                    partial_send, partial_recv.at[c], device({e: move}, 0),
                )

    def relay_partials(c):
        whole(far_in, c * LANES, LANES, far_recv.at[c])
        for s, move in enumerate((1, 3)):
            at = pl.ds(partial_row(c, s) + s * half, half)
            partial_out[at, :] = partial_out[at, :] + far_in[pl.ds(c * LANES + s * half, half), :]
            remote(
                partial_out.at[at], partial_in.at[at],
                partial_send, partial_recv.at[c], device({AXES[c % 3][2]: move}, 0),
            )

    for c in range(UNITS):
        unpack(c)
        if c >= 3:
            relay_partials(c - 3)
    for c in range(UNITS - 3, UNITS):
        relay_partials(c)
    for c in range(UNITS):
        whole(partial_in, partial_row(c, 0), 2 * LANES, partial_recv.at[c])
        regroup[pl.ds(c, LANES, stride=PITCH), :] = (
            own_sum[pl.ds(c * LANES, LANES), :]
            + partial_in[pl.ds(partial_row(c, 0), LANES), :]
            + partial_in[pl.ds(partial_row(c, 1), LANES), :]
        )
    loads[4].wait()
    for xo in range(tile_rows):
        parts = [
            regroup[pl.ds((xo * tile_cols + yo) * PITCH, UNITS), :] for yo in range(tile_cols)
        ]
        for g, value in enumerate(block_transpose(parts)):
            pushed_ref[g // 2, pl.ds(xo * TS + (g % 2) * 8, 8), :] = value

    ends = jnp.zeros((8, cy), F32)
    for z in range(planes):
        both = jnp.concatenate(split2(target[z] - pushed_ref[z]), axis=1)
        halves[z] = both
        value = dot(xends_tab[z], both)
        ends += value[:8, :cy] + (value[:8, cy:] + value[8:, :cy])
    xmsg[...] = ends
    for s in range(4):
        for h in range(2):
            if s + h:
                remote(xmsg, xall.at[p], x_send, x_recv, device({1: s}, h))
    xall[p] = ends
    y_ends = jnp.zeros((8, cx), F32)
    for z in range(planes):
        both = halves[z]
        value = dot(xtab_hi[z], both)
        value = value[:, :cy] + (value[:, cy:] + dot(xtab_lo[z], both[:, :cy]))
        smooth[z] = value
        value = dot(yends_tab[z], jnp.concatenate(split2(value), axis=0), ((1,), (1,)))
        y_ends += value[:8, :cx] + (value[:8, cx:] + value[8:, :cx])
    whole(xall, 0, n_gx - 1, x_recv)
    flow = inflow(0, n_gx, xall, cy)
    at_last = jnp.sum(flow * last_rows, axis=1, keepdims=True)
    at_first = jnp.sum(flow * first_rows, axis=1, keepdims=True)
    upper = row8 < planes
    entered = jnp.where(upper, at_last, pltpu.roll(jnp.broadcast_to(at_first, (8, LANES)), 4, 0)[:, 0:1])
    left = jnp.where(upper, pltpu.roll(jnp.broadcast_to(at_last, (8, LANES)), 4, 0)[:, 0:1], at_first)
    y_ends += edge_rows[0] * entered + edge_rows[1] * left
    ymsg[...] = y_ends
    for dz in range(4):
        for dx in range(4):
            if dz + dx:
                remote(ymsg, yall.at[q], y_send, y_recv, device({2: dz, 0: dx}, 0))
    yall[q] = y_ends

    loads[5].wait()
    for z in range(planes):
        value = smooth[z] + (
            xfill[z] * flow[z : z + 1] + xfill[planes + z] * flow[planes + z : planes + z + 1]
        )
        potential[z] = potential[z] + dot3(split2(value), (ytab_hi[z], ytab_lo[z]))
    whole(yall, 0, n_gy - 1, y_recv)
    flow = inflow(2 * n_gx, n_gy, yall, cx)
    hi = flow.astype(BF16).astype(F32)
    flow = jnp.concatenate([hi, flow - hi, hi, flow - hi], axis=0).astype(BF16)
    for z in range(planes):
        next_ref[z] = potential[z] + dot(flow, yfill_tab[z], ((0,), (0,)))

    whole(metas, 0, 9, meta_send)
    whole(spread_in, 0, 3 * UNITS * LANES, spread_send)
    whole(slots_out, 0, 7 * UNITS * BLOCK, slot_send)
    whole(labels_out, 0, 21, label_send)
    whole(far_out, 0, UNITS * LANES, far_send)
    whole(partial_out, 0, 2 * UNITS * LANES, partial_send)
    whole(xall, 0, n_gx - 1, x_send)
    whole(yall, 0, n_gy - 1, y_send)


def per_device(source_mass, target_density, potential, dest_device, dest_tile, mass_counts, reach):
    planes, cx, cy = source_mass.shape

    def lanes(a):
        return jnp.swapaxes(a.reshape(a.shape[2:]), 0, 1)

    hbm = pl.BlockSpec(memory_space=pl.ANY)
    dma = pltpu.SemaphoreType.DMA
    vmem = pltpu.VMEM
    grid = jax.ShapeDtypeStruct((planes, cx, cy), F32)
    field = vmem((planes, cx, cy), F32)

    def rows(count):
        return vmem((count, LANES), F32)

    return pl.pallas_call(
        kernel,
        out_shape=(grid, grid),
        in_specs=[hbm] * 7,
        out_specs=(pl.BlockSpec(memory_space=vmem), pl.BlockSpec(memory_space=vmem)),
        scratch_shapes=[
            field, field, field, field,
            pltpu.SMEM((planes,), F32),
            vmem((3, 4, LANES), jnp.int32),
            vmem((9, 3, 4, LANES), jnp.int32),
            rows(UNITS * LANES), rows(LANES * PITCH + 16), rows(3 * UNITS * LANES),
            vmem((12, 256, LANES), BF16),
            vmem((12, 256, LANES), F32),
            vmem((3, 8 * LANES, LANES), F32),
            rows(7 * UNITS * BLOCK + 8), rows(8 * UNITS * BLOCK + 8),
            vmem((24, 1, LANES), F32),
            vmem((24, 1, LANES), F32),
            rows(UNITS * LANES), rows(UNITS * LANES),
            rows(2 * UNITS * LANES), rows(2 * UNITS * LANES), rows(UNITS * LANES),
            vmem((planes, cx, cx), BF16),
            vmem((planes, cx, cx), BF16),
            vmem((planes, cy, cy), BF16),
            vmem((planes, cy, cy), BF16),
            vmem((planes, 16, cx), BF16),
            vmem((planes, 16, cy), BF16),
            vmem((2 * planes, cx, LANES), F32),
            vmem((planes, 32, cy), BF16),
            vmem((48, 8, LANES), F32),
            vmem((2, 8, cx), F32),
            vmem((planes, cx, 2 * cy), BF16),
            vmem((8, cy), F32),
            vmem((8, 8, cy), F32),
            vmem((8, cx), F32),
            vmem((16, 8, cx), F32),
            dma((7,)), dma, dma((3,)), dma, dma((UNITS,)), dma((UNITS,)),
            dma, dma((UNITS,)), dma, dma((3,)), dma, dma((UNITS,)),
            dma, dma((UNITS,)), dma, dma, dma, dma,
        ],
        compiler_params=pltpu.CompilerParams(collective_id=0, has_side_effects=True),
        name="dual_step",
    )(
        source_mass, target_density, potential,
        lanes(dest_device), lanes(dest_tile), lanes(mass_counts), reach,
    )


def solution(mesh):
    in_specs = (
        P(None, "gx", "gy"),
        P(None, "gx", "gy"),
        P(None, "gx", "gy"),
        P("gx", "gy", None, None),
        P("gx", "gy", None, None),
        P("gx", "gy", None, None),
        P(),
    )
    out_specs = (P(None, "gx", "gy"), P(None, "gx", "gy"))
    return jax.shard_map(
        per_device, mesh=mesh, in_specs=in_specs, out_specs=out_specs, check_vma=False
    )
```

time: 55.3 us -> 56.2 us (1.016)
  Pallas kernels: 51.8 us -> 52.6 us
    pallas_call x1, Pallas kernels: 51.8 us -> 52.6 us  [per_device(): pl.pallas_call(kernel, out_shape=(grid, grid), in_specs=[hbm] * 7, out_sp...]
where the time goes in v3:
time: 56.2 us; the launch traced here: 56 us
  Pallas kernels  52.6 us (94%)
  local copies, waits for them, and re-layouts  2.72 us (5%)
  between operations  0.65 us (1%)
    pallas_call x1, Pallas kernels, per_device(): pl.pallas_call(kernel, out_shape=(grid, grid), in_specs=[hbm] * 7, out_sp...  52.6 us
    unnamed x4, local copies, waits for them, and re-layouts  2.72 us

profile of v3, /device:TPU:0, one launch (start us, length us, event | category | flops | bytes accessed | tf_op | source)
XLA Modules:
  0.0 56.0 jit_solution(10717651625929378000)
XLA Ops:
  0.6 52.6 %dual_step.1 = (f32[4,256,128]{2,1,0:T(8,128)}, f32[4,256,128]{2,1,0:T(8,128)}) custom-call(f32[4,256,128]{2,1,0:T(8,128)} %source_ref.1, f32[4,256,128]{2,1,0:T(8,128)} %target_ref.1, f32[4,256,128]{2,1,0:T(8,128)} %potential_ref.1, s32[4,128]{1,0:T(4,128)} %bitcast.9, s32[4,128]{1,0:T(4,128)} %bitcast.10, s32[4,128]{1,0:T(4,128)} %bitcast.11, f32[4]{0:T(128)} %reach_hbm.1), custom_call_target="tpu_custom_call" | custom-call | tf_op jit(solution)/shard_map/dual_step/pallas_call | solution.py:522
  53.3 0.0 copy-start
  53.3 1.9 %copy.11 = f32[4,256,128]{2,1,0:T(8,128)} copy(f32[4,256,128]{2,1,0:T(8,128)} %get-tuple-element.4) | data formatting | bytes 1048576
  55.2 0.0 copy-done
  55.2 0.8 %copy.12 = f32[4,256,128]{2,1,0:T(8,128)} copy(f32[4,256,128]{2,1,0:T(8,128)S(1)} %copy-done) | data formatting | bytes 1048576
Async XLA Ops:
  53.3 1.9 %copy-start = (f32[4,256,128]{2,1,0:T(8,128)S(1)}, f32[4,256,128]{2,1,0:T(8,128)}, u32[]{:S(2)}) copy-start(f32[4,256,128]{2,1,0:T(8,128)} %get-tuple-element.5) | copy-start | bytes 1572868

commit v4 on v3

--- a/solution.py
+++ b/solution.py
@@ -75,18 +75,17 @@
     natural, target, potential, smooth, reach_ref,
     meta, metas, tiles, regroup, spread_in, picks, weights, places,
     slots_out, slots_in, labels_out, labels_in,
-    far_out, far_in, partial_out, partial_in, own_sum,
+    partial_out, partial_in, own_sum,
     xtab_hi, xtab_lo, ytab_hi, ytab_lo, xends_tab, yends_tab, xfill, yfill_tab,
     coef, edge_rows, halves, xmsg, xall, ymsg, yall,
-    load_sem, meta_send, meta_recv, spread_send, spread_recv, relay_recv,
-    slot_send, slot_recv, label_send, label_recv, far_send, far_recv,
+    load_sem, meta_send, meta_recv, spread_send, spread_recv,
+    slot_send, slot_recv, label_send, label_recv,
     partial_send, partial_recv, x_send, x_recv, y_send, y_recv,
 ):
     p, q = lax.axis_index("gx"), lax.axis_index("gy")
     n_gx, n_gy = 8, 16
     planes, cx, cy = source_ref.shape
     tile_rows, tile_cols = cx // TS, cy // TS
-    half = LANES // 2
     here = (q & 3, p >> 1, q >> 2)
     core = p & 1
     stride = (1, 2 * n_gy, 4)
@@ -132,28 +131,124 @@
         tiles[pl.ds(c * LANES, LANES), :] = regroup[pl.ds(c, LANES, stride=PITCH), :]
     pl.semaphore_wait(barrier, len(peers))
 
-    def spread_row(c, s):
-        return (c * 3 + s) * LANES
-
     for g, (a, _, _) in enumerate(AXES):
         for s in range(1, 4):
             remote(meta, metas.at[g * 3 + s - 1], meta_send, meta_recv.at[g], device({a: s}, 0))
     for c in range(UNITS):
-        for s, move in enumerate((1, 3)):
+        for s in range(1, 4):
             remote(
                 tiles.at[pl.ds(c * LANES, LANES)],
-                spread_in.at[pl.ds(spread_row(c, s), LANES)],
-                spread_send, spread_recv.at[c], device({AXES[c % 3][0]: move}, 0),
-            )
-
-    def relay_tiles(c):
-        whole(spread_in, spread_row(c, 0), 2 * LANES, spread_recv.at[c])
-        for s, move in enumerate((1, 3)):
-            remote(
-                spread_in.at[pl.ds(spread_row(c, s) + s * half, half)],
-                spread_in.at[pl.ds(spread_row(c, 2) + s * half, half)],
-                spread_send, relay_recv.at[c], device({AXES[c % 3][0]: move}, 0),
-            )
+                spread_in.at[pl.ds((c * 3 + s - 1) * LANES, LANES)],
+                spread_send, spread_recv.at[c], device({AXES[c % 3][0]: s}, 0),
+            )
+
+    loads[6].wait()
+    decay = [jnp.full((1, 1), 1.0 - 1.0 / reach_ref[z], F32) for z in range(planes)]
+    logs = [jnp.log(d) for d in decay]
+    scale = [(1.0 - d) ** 2 for d in decay]
+    row8 = iota((8, 1), 0)
+
+    def both_rows(values):
+        result = jnp.zeros((8, values[0].shape[1]), F32)
+        for z, v in enumerate(values):
+            result = jnp.where((row8 == z) | (row8 == planes + z), v, result)
+        return result
+
+    def stacked(a):
+        hi = a.astype(BF16).astype(F32)
+        return jnp.concatenate([hi, a - hi], axis=0).astype(BF16)
+
+    logs8, scale8 = both_rows(logs), both_rows(scale)
+
+    def rows_of(n):
+        at = iota((8, n), 1)
+        squares = powers(2.0 * logs8, at)
+        hi = squares.astype(BF16).astype(F32)
+        mid = (squares - hi).astype(BF16).astype(F32)
+        parts = jnp.concatenate([hi, mid, squares - hi - mid, jnp.zeros_like(hi)], axis=0)
+        inside = (iota((n, n), 0) + iota((n, n), 1) < n).astype(BF16)
+        sums = dot(parts.astype(BF16), inside)
+        sums = sums[0:8] + (sums[8:16] + sums[16:24])
+        last = powers(logs8, n - 1 - at)
+        fall = powers(logs8, n - at)
+        first = scale8 * powers(logs8, at) * sums
+        swept = scale8 * powers(logs8, at + 1) * sums
+        return sums, last, first, swept, fall
+
+    upper = row8 < planes
+    sums_x, last_x, first_x, swept_x, fall_x = rows_of(cx)
+    sums_y, last_rows, first_rows, swept_y, fall_y = rows_of(cy)
+    edge_rows[0], edge_rows[1] = swept_x, fall_x
+    spare = jnp.zeros((cy - 24, cx), F32)
+    columns = jnp.transpose(
+        jnp.concatenate(
+            [sums_x, jnp.where(upper, swept_x, fall_x),
+             jnp.concatenate([sums_y, sums_y], axis=1), spare],
+            axis=0,
+        )
+    )
+    across_row = iota((cy, cy), 0)
+    gap = across_row - iota((cy, cy), 1)
+    for z in range(planes):
+        near = powers(logs[z], jnp.abs(gap)) * scale[z]
+        below = powers(logs[z], gap + cy) * scale[z]
+        above = powers(logs[z], cy - gap) * scale[z]
+
+        def column(i, first, count):
+            return jnp.broadcast_to(columns[first : first + count, i : i + 1], (count, cy))
+
+        low = gap >= 0
+        g0, g1, gy = column(z, 0, cy), column(z, cy, cy), column(16 + z, 0, cy)
+        r0, r1, ry = sums_x[z : z + 1, :cy], sums_x[z : z + 1, cy:], sums_y[z : z + 1]
+        for r, (left_part, right_part) in enumerate([
+            (near * jnp.where(low, g0, r0), above * r1),
+            (below * g1, near * jnp.where(low, g1, r1)),
+        ]):
+            at = pl.ds(r * cy, cy)
+            for w, part in enumerate((left_part, right_part)):
+                hi, lo = split2(part)
+                xtab_hi[z, at, pl.ds(w * cy, cy)] = hi
+                xtab_lo[z, at, pl.ds(w * cy, cy)] = lo
+        ytab_hi[z], ytab_lo[z] = split2(near * jnp.where(low, gy, ry))
+        xfill[z] = jnp.broadcast_to(columns[:, 8 + z : 9 + z], (cx, LANES))
+        xfill[planes + z] = jnp.broadcast_to(
+            columns[:, 8 + planes + z : 9 + planes + z], (cx, LANES)
+        )
+        one, two = row8 == z, row8 == planes + z
+        xends_tab[z] = stacked(jnp.where(one, last_x, 0.0) + jnp.where(two, first_x, 0.0))
+        yends_tab[z] = stacked(jnp.where(one, last_rows, 0.0) + jnp.where(two, first_rows, 0.0))
+        fill = jnp.where(one, swept_y, 0.0) + jnp.where(two, fall_y, 0.0)
+        hi = fill.astype(BF16).astype(F32)
+        yfill_tab[z] = jnp.concatenate([hi, hi, fill - hi, fill - hi], axis=0).astype(BF16)
+
+    def coefficients(base, count, at, n, first):
+        across = jnp.exp(float(n) * logs8)
+        powers_of = [jnp.ones((8, 1), F32)]
+        for _ in range(count - 1):
+            powers_of.append(powers_of[-1] * across)
+        low = row8 < planes
+        before, after = [], []
+        for i in range(count):
+            coming = jnp.zeros((8, 1), F32)
+            going = jnp.zeros((8, 1), F32)
+            for m in range(count - 1):
+                coming = jnp.where(at - 1 - i == m, powers_of[m], coming)
+                going = jnp.where(i - at - 1 == m, powers_of[m], going)
+            before.append(coming)
+            after.append(going)
+        through = jnp.zeros((8, 1), F32)
+        crossing = [None] * count
+        for i in reversed(range(count)):
+            crossing[i] = first * through
+            through = after[i] + across * through
+        for i in range(count):
+            coef[base + i] = jnp.broadcast_to(jnp.where(low, before[i], after[i]), (8, LANES))
+            coef[base + count + i] = jnp.broadcast_to(
+                jnp.where(low, crossing[i], 0.0), (8, LANES)
+            )
+
+    coefficients(0, n_gx, p, cx, swept_x[:, 0:1])
+    coefficients(2 * n_gx, n_gy, q, cy, swept_y[:, 0:1])
 
     earlier = (iota((LANES, LANES), 0) < iota((LANES, LANES), 1)).astype(BF16)
     row = iota((32, LANES), 0)
@@ -190,8 +285,6 @@
             )
         picks[g * 4 + s] = jnp.concatenate(found, axis=0).astype(BF16)
 
-    source_meta = (None, 0, 2, 1)
-
     def find_labels(g):
         b = AXES[g][1]
         for ih in range(8):
@@ -216,24 +309,19 @@
     for g in range(3):
         whole(metas, g * 3, 3, meta_recv.at[g])
         for s in range(1, 4):
-            find_slots(g, s, metas[g * 3 + source_meta[s]])
-        for c in range(g, UNITS, 3)[:1]:
-            relay_tiles(c)
-    for g in range(3):
+            find_slots(g, s, metas[g * 3 + s - 1])
         find_labels(g)
-    for c in range(3, UNITS):
-        relay_tiles(c)
 
     def pack(c):
         g = c % 3
         b = AXES[g][1]
         for s in range(4):
-            if s == 3:
-                whole(spread_in, spread_row(c, 2), LANES, relay_recv.at[c])
+            if s == 1:
+                whole(spread_in, c * 3 * LANES, 3 * LANES, spread_recv.at[c])
             if s == 0:
                 value = tiles[pl.ds(c * LANES, LANES), :]
             else:
-                value = spread_in[pl.ds(spread_row(c, s - 1), LANES), :]
+                value = spread_in[pl.ds((c * 3 + s - 1) * LANES, LANES), :]
             pick = picks[g * 4 + s]
             value = dot(
                 jnp.concatenate([pick, pick], axis=1), jnp.concatenate(split2(value), axis=0)
@@ -256,93 +344,6 @@
 
     for c in range(UNITS):
         pack(c)
-
-    loads[6].wait()
-    decay = [jnp.full((1, 1), 1.0 - 1.0 / reach_ref[z], F32) for z in range(planes)]
-    logs = [jnp.log(d) for d in decay]
-    scale = [(1.0 - d) ** 2 for d in decay]
-    row8 = iota((8, 1), 0)
-
-    def both_rows(values):
-        result = jnp.zeros((8, values[0].shape[1]), F32)
-        for z, v in enumerate(values):
-            result = jnp.where((row8 == z) | (row8 == planes + z), v, result)
-        return result
-
-    def stacked(a):
-        hi = a.astype(BF16).astype(F32)
-        return jnp.concatenate([hi, a - hi], axis=0).astype(BF16)
-
-    swept_first, last_rows, first_rows = {}, {}, {}
-    for axis, n in (("x", cx), ("y", cy)):
-        at = iota((1, n), 1)
-        gap = iota((n, n), 0) - iota((n, n), 1)
-        lasts, firsts, swepts, falls = [], [], [], []
-        for z in range(planes):
-            lower = jnp.where(gap >= 0, powers(logs[z], jnp.maximum(gap, 0)), 0.0)
-            both = scale[z] * dot_f32(lower, lower, ((0,), (0,)))
-            last = powers(logs[z], n - 1 - at)
-            rise = powers(logs[z], at + 1)
-            fall = powers(logs[z], n - at)
-            swept = scale[z] * dot_f32(jnp.broadcast_to(rise, (8, n)), lower)[0:1]
-            lasts.append(last)
-            firsts.append(both[0:1])
-            swepts.append(swept)
-            falls.append(fall)
-            ends = jnp.where(row8 == z, last, 0.0) + jnp.where(
-                row8 == planes + z, both[0:1], 0.0
-            )
-            if axis == "x":
-                xtab_hi[z], xtab_lo[z] = split2(both)
-                xends_tab[z] = stacked(ends)
-                down = iota((n, LANES), 0)
-                xfill[z] = scale[z] * dot_f32(lower, powers(logs[z], down + 1), ((0,), (0,)))
-                xfill[planes + z] = powers(logs[z], n - down)
-            else:
-                ytab_hi[z], ytab_lo[z] = split2(both)
-                yends_tab[z] = stacked(ends)
-                fill = jnp.where(row8 == z, swept, 0.0) + jnp.where(
-                    row8 == planes + z, fall, 0.0
-                )
-                hi = fill.astype(BF16).astype(F32)
-                yfill_tab[z] = jnp.concatenate([hi, hi, fill - hi, fill - hi], axis=0).astype(
-                    BF16
-                )
-        swept_first[axis] = both_rows([v[:, 0:1] for v in swepts])
-        if axis == "x":
-            edge_rows[0] = both_rows(swepts)
-            edge_rows[1] = both_rows(falls)
-        else:
-            last_rows, first_rows = both_rows(lasts), both_rows(firsts)
-
-    def coefficients(base, count, at, n, first):
-        across = both_rows([powers(logs[z], jnp.full((1, 1), n, jnp.int32)) for z in range(planes)])
-        powers_of = [jnp.ones((8, 1), F32)]
-        for _ in range(count - 1):
-            powers_of.append(powers_of[-1] * across)
-        low = row8 < planes
-        before, after = [], []
-        for i in range(count):
-            coming = jnp.zeros((8, 1), F32)
-            going = jnp.zeros((8, 1), F32)
-            for m in range(count - 1):
-                coming = jnp.where(at - 1 - i == m, powers_of[m], coming)
-                going = jnp.where(i - at - 1 == m, powers_of[m], going)
-            before.append(coming)
-            after.append(going)
-        through = jnp.zeros((8, 1), F32)
-        crossing = [None] * count
-        for i in reversed(range(count)):
-            crossing[i] = first * through
-            through = after[i] + across * through
-        for i in range(count):
-            coef[base + i] = jnp.broadcast_to(jnp.where(low, before[i], after[i]), (8, LANES))
-            coef[base + count + i] = jnp.broadcast_to(
-                jnp.where(low, crossing[i], 0.0), (8, LANES)
-            )
-
-    coefficients(0, n_gx, p, cx, swept_first["x"])
-    coefficients(2 * n_gx, n_gy, q, cy, swept_first["y"])
 
     def inflow(base, count, all_ref, width):
         columns = []
@@ -379,9 +380,6 @@
             row_of.append((tile_index == named).astype(BF16))
         selects.append(row_of)
 
-    def partial_row(c, s):
-        return (c * 2 + s) * LANES
-
     def unpack(c):
         g = c % 3
         e = AXES[g][2]
@@ -398,46 +396,22 @@
             value = value[:, :LANES] + value[:, LANES:]
             if j == 0:
                 own_sum[pl.ds(c * LANES, LANES), :] = value
-            elif j == 2:
-                far_out[pl.ds(c * LANES, LANES), :] = value
-                for s, move in enumerate((1, 3)):
-                    remote(
-                        far_out.at[pl.ds(c * LANES + s * half, half)],
-                        far_in.at[pl.ds(c * LANES + s * half, half)],
-                        far_send, far_recv.at[c], device({e: move}, 0),
-                    )
             else:
-                s, move = (0, 1) if j == 1 else (1, 3)
-                partial_out[pl.ds(partial_row(c, s), LANES), :] = value
-                at = pl.ds(partial_row(c, s) + (1 - s) * half, half)
+                at = pl.ds((c * 3 + j - 1) * LANES, LANES)
+                partial_out[at, :] = value
                 remote(
                     partial_out.at[at], partial_in.at[at],
-                    partial_send, partial_recv.at[c], device({e: move}, 0),
+                    partial_send, partial_recv.at[c], device({e: j}, 0),
                 )
-
-    def relay_partials(c):
-        whole(far_in, c * LANES, LANES, far_recv.at[c])
-        for s, move in enumerate((1, 3)):
-            at = pl.ds(partial_row(c, s) + s * half, half)
-            partial_out[at, :] = partial_out[at, :] + far_in[pl.ds(c * LANES + s * half, half), :]
-            remote(
-                partial_out.at[at], partial_in.at[at],
-                partial_send, partial_recv.at[c], device({AXES[c % 3][2]: move}, 0),
-            )
 
     for c in range(UNITS):
         unpack(c)
-        if c >= 3:
-            relay_partials(c - 3)
-    for c in range(UNITS - 3, UNITS):
-        relay_partials(c)
     for c in range(UNITS):
-        whole(partial_in, partial_row(c, 0), 2 * LANES, partial_recv.at[c])
-        regroup[pl.ds(c, LANES, stride=PITCH), :] = (
-            own_sum[pl.ds(c * LANES, LANES), :]
-            + partial_in[pl.ds(partial_row(c, 0), LANES), :]
-            + partial_in[pl.ds(partial_row(c, 1), LANES), :]
-        )
+        whole(partial_in, c * 3 * LANES, 3 * LANES, partial_recv.at[c])
+        total = own_sum[pl.ds(c * LANES, LANES), :]
+        for j in range(3):
+            total += partial_in[pl.ds((c * 3 + j) * LANES, LANES), :]
+        regroup[pl.ds(c, LANES, stride=PITCH), :] = total
     loads[4].wait()
     for xo in range(tile_rows):
         parts = [
@@ -470,7 +444,6 @@
     flow = inflow(0, n_gx, xall, cy)
     at_last = jnp.sum(flow * last_rows, axis=1, keepdims=True)
     at_first = jnp.sum(flow * first_rows, axis=1, keepdims=True)
-    upper = row8 < planes
     entered = jnp.where(upper, at_last, pltpu.roll(jnp.broadcast_to(at_first, (8, LANES)), 4, 0)[:, 0:1])
     left = jnp.where(upper, pltpu.roll(jnp.broadcast_to(at_last, (8, LANES)), 4, 0)[:, 0:1], at_first)
     y_ends += edge_rows[0] * entered + edge_rows[1] * left
@@ -498,8 +471,7 @@
     whole(spread_in, 0, 3 * UNITS * LANES, spread_send)
     whole(slots_out, 0, 7 * UNITS * BLOCK, slot_send)
     whole(labels_out, 0, 21, label_send)
-    whole(far_out, 0, UNITS * LANES, far_send)
-    whole(partial_out, 0, 2 * UNITS * LANES, partial_send)
+    whole(partial_out, 0, 3 * UNITS * LANES, partial_send)
     whole(xall, 0, n_gx - 1, x_send)
     whole(yall, 0, n_gy - 1, y_send)
 
@@ -536,8 +508,7 @@
             rows(7 * UNITS * BLOCK + 8), rows(8 * UNITS * BLOCK + 8),
             vmem((24, 1, LANES), F32),
             vmem((24, 1, LANES), F32),
-            rows(UNITS * LANES), rows(UNITS * LANES),
-            rows(2 * UNITS * LANES), rows(2 * UNITS * LANES), rows(UNITS * LANES),
+            rows(3 * UNITS * LANES), rows(3 * UNITS * LANES), rows(UNITS * LANES),
             vmem((planes, cx, cx), BF16),
             vmem((planes, cx, cx), BF16),
             vmem((planes, cy, cy), BF16),
@@ -553,15 +524,20 @@
             vmem((8, 8, cy), F32),
             vmem((8, cx), F32),
             vmem((16, 8, cx), F32),
-            dma((7,)), dma, dma((3,)), dma, dma((UNITS,)), dma((UNITS,)),
+            dma((7,)), dma, dma((3,)), dma, dma((UNITS,)),
             dma, dma((UNITS,)), dma, dma((3,)), dma, dma((UNITS,)),
-            dma, dma((UNITS,)), dma, dma, dma, dma,
+            dma, dma, dma, dma,
         ],
-        compiler_params=pltpu.CompilerParams(collective_id=0, has_side_effects=True),
+        compiler_params=pltpu.CompilerParams(collective_id=0, has_side_effects=True, vmem_limit_bytes=40 * 1024 * 1024),
         name="dual_step",
     )(
-        source_mass, target_density, potential,
-        lanes(dest_device), lanes(dest_tile), lanes(mass_counts), reach,
+        *[
+            pltpu.with_memory_space_constraint(a, pltpu.HBM)
+            for a in (
+                source_mass, target_density, potential,
+                lanes(dest_device), lanes(dest_tile), lanes(mass_counts), reach,
+            )
+        ],
     )
 
 

time: 56.2 us -> 50 us (0.89)
  Pallas kernels: 52.6 us -> 47.3 us
  local copies, waits for them, and re-layouts: 2.72 us -> 1.59 us
    pallas_call x1, Pallas kernels: 52.6 us -> 47.3 us  [per_device(): pl.pallas_call(kernel, out_shape=(grid, grid), in_specs=[hbm] * 7, out_sp...]
    unnamed x4 -> x2, local copies, waits for them, and re-layouts: 2.72 us -> 1.59 us
where the time goes in v4:
time: 50 us; the launch traced here: 49.6 us
  Pallas kernels  47.3 us (95%)
  local copies, waits for them, and re-layouts  1.59 us (3%)
  between operations  0.64 us (1%)
    pallas_call x1, Pallas kernels, per_device(): pl.pallas_call(kernel, out_shape=(grid, grid), in_specs=[hbm] * 7, out_sp...  47.3 us
    unnamed x2, local copies, waits for them, and re-layouts  1.59 us

profile of v4, /device:TPU:0, one launch (start us, length us, event | category | flops | bytes accessed | tf_op | source)
XLA Modules:
  0.0 49.6 jit_solution(13611667163413318550)
XLA Ops:
  0.6 47.3 %dual_step.1 = (f32[4,256,128]{2,1,0:T(8,128)S(1)}, f32[4,256,128]{2,1,0:T(8,128)S(1)}) custom-call(f32[4,256,128]{2,1,0:T(8,128)} %source_ref.1, f32[4,256,128]{2,1,0:T(8,128)} %target_ref.1, f32[4,256,128]{2,1,0:T(8,128)} %potential_ref.1, s32[4,128]{1,0:T(4,128)} %bitcast.9, s32[4,128]{1,0:T(4,128)} %bitcast.10, s32[4,128]{1,0:T(4,128)} %bitcast.11, ...), custom_call_target="tpu_custom_call" | custom-call | tf_op jit(solution)/shard_map/dual_step/pallas_call | solution.py:494
  48.0 0.8 %copy.11 = f32[4,256,128]{2,1,0:T(8,128)} copy(f32[4,256,128]{2,1,0:T(8,128)S(1)} %get-tuple-element.4) | data formatting | bytes 1048576
  48.8 0.8 %copy.12 = f32[4,256,128]{2,1,0:T(8,128)} copy(f32[4,256,128]{2,1,0:T(8,128)S(1)} %get-tuple-element.5) | data formatting | bytes 1048576

commit v5 on v4

--- a/solution.py
+++ b/solution.py
@@ -13,6 +13,7 @@
 AXES = ((0, 1, 2), (1, 2, 0), (2, 0, 1))
 GROUP = SLOTS * 4
 BLOCK = 4 * GROUP
+EARLY = 5
 PITCH = 9
 F32 = jnp.float32
 BF16 = jnp.bfloat16
@@ -79,7 +80,7 @@
     xtab_hi, xtab_lo, ytab_hi, ytab_lo, xends_tab, yends_tab, xfill, yfill_tab,
     coef, edge_rows, halves, xmsg, xall, ymsg, yall,
     load_sem, meta_send, meta_recv, spread_send, spread_recv,
-    slot_send, slot_recv, label_send, label_recv,
+    slot_send, slot_recv, own_recv, label_send, label_recv,
     partial_send, partial_recv, x_send, x_recv, y_send, y_recv,
 ):
     p, q = lax.axis_index("gx"), lax.axis_index("gy")
@@ -100,12 +101,14 @@
             device_id=to, device_id_type=MESH,
         ).start()
 
+    split = [pl.ds(r * (cx // 2), cx // 2) for r in range(2)]
     loads = [
         pltpu.make_async_copy(a, b, load_sem.at[i])
         for i, (a, b) in enumerate([
+            (source_ref.at[:, split[0]], natural.at[:, split[0]]),
+            (source_ref.at[:, split[1]], natural.at[:, split[1]]),
             (device_ref, meta.at[0]), (tile_ref, meta.at[1]), (count_ref, meta.at[2]),
-            (source_ref, natural), (target_ref, target), (potential_ref, potential),
-            (reach_hbm, reach_ref),
+            (reach_hbm, reach_ref), (target_ref, target), (potential_ref, potential),
         ])
     ]
     for load in loads:
@@ -119,30 +122,30 @@
             barrier, inc=1, device_id=device(moves, other), device_id_type=MESH
         )
 
-    for load in loads[:4]:
-        load.wait()
     for xo in range(tile_rows):
+        if xo % (tile_rows // 2) == 0:
+            loads[xo // (tile_rows // 2)].wait()
         parts = [
             natural[g // 2, pl.ds(xo * TS + (g % 2) * 8, 8), :] for g in range(2 * planes)
         ]
         for yo, value in enumerate(block_transpose(parts)):
             regroup[pl.ds((xo * tile_cols + yo) * PITCH, UNITS), :] = value
-    for c in range(UNITS):
-        tiles[pl.ds(c * LANES, LANES), :] = regroup[pl.ds(c, LANES, stride=PITCH), :]
+    for load in loads[2:5]:
+        load.wait()
     pl.semaphore_wait(barrier, len(peers))
-
     for g, (a, _, _) in enumerate(AXES):
         for s in range(1, 4):
             remote(meta, metas.at[g * 3 + s - 1], meta_send, meta_recv.at[g], device({a: s}, 0))
     for c in range(UNITS):
-        for s in range(1, 4):
+        tiles[pl.ds(c * LANES, LANES), :] = regroup[pl.ds(c, LANES, stride=PITCH), :]
+        for s in (2, 1, 3):
             remote(
                 tiles.at[pl.ds(c * LANES, LANES)],
                 spread_in.at[pl.ds((c * 3 + s - 1) * LANES, LANES)],
                 spread_send, spread_recv.at[c], device({AXES[c % 3][0]: s}, 0),
             )
 
-    loads[6].wait()
+    loads[5].wait()
     decay = [jnp.full((1, 1), 1.0 - 1.0 / reach_ref[z], F32) for z in range(planes)]
     logs = [jnp.log(d) for d in decay]
     scale = [(1.0 - d) ** 2 for d in decay]
@@ -314,7 +317,6 @@
 
     def pack(c):
         g = c % 3
-        b = AXES[g][1]
         for s in range(4):
             if s == 1:
                 whole(spread_in, c * 3 * LANES, 3 * LANES, spread_recv.at[c])
@@ -335,11 +337,14 @@
                     slots_in[pl.ds(c * 8 * BLOCK + within, SLOTS), :] = piece
                 else:
                     slots_out[pl.ds((c * 7 + ih - 1) * BLOCK + within, SLOTS), :] = piece
+        send_slots(c, GROUP, BLOCK - GROUP, slot_recv)
+
+    def send_slots(c, first, count, recv):
         for ih in range(1, 8):
             remote(
-                slots_out.at[pl.ds((c * 7 + ih - 1) * BLOCK, BLOCK)],
-                slots_in.at[pl.ds((c * 8 + ih) * BLOCK, BLOCK)],
-                slot_send, slot_recv.at[c], device({b: ih // 2}, ih % 2),
+                slots_out.at[pl.ds((c * 7 + ih - 1) * BLOCK + first, count)],
+                slots_in.at[pl.ds((c * 8 + ih) * BLOCK + first, count)],
+                slot_send, recv.at[c], device({AXES[c % 3][1]: ih // 2}, ih % 2),
             )
 
     for c in range(UNITS):
@@ -380,39 +385,37 @@
             row_of.append((tile_index == named).astype(BF16))
         selects.append(row_of)
 
-    def unpack(c):
-        g = c % 3
-        e = AXES[g][2]
-        whole(slots_in, (c * 8 + 1) * BLOCK, 7 * BLOCK, slot_recv.at[c])
-        for j in (2, 1, 3, 0):
-            rows = jnp.concatenate(
-                [
-                    slots_in[pl.ds((c * 8 + ih) * BLOCK + j * GROUP, GROUP), :]
-                    for ih in range(8)
-                ],
-                axis=0,
-            )
-            value = dot(selects[g][j], jnp.concatenate(split2(rows), axis=1))
-            value = value[:, :LANES] + value[:, LANES:]
-            if j == 0:
-                own_sum[pl.ds(c * LANES, LANES), :] = value
-            else:
-                at = pl.ds((c * 3 + j - 1) * LANES, LANES)
-                partial_out[at, :] = value
-                remote(
-                    partial_out.at[at], partial_in.at[at],
-                    partial_send, partial_recv.at[c], device({e: j}, 0),
-                )
+    def collect(c, j):
+        rows = jnp.concatenate(
+            [slots_in[pl.ds((c * 8 + ih) * BLOCK + j * GROUP, GROUP), :] for ih in range(8)],
+            axis=0,
+        )
+        value = dot(selects[c % 3][j], jnp.concatenate(split2(rows), axis=1))
+        return value[:, :LANES] + value[:, LANES:]
 
     for c in range(UNITS):
-        unpack(c)
+        whole(slots_in, (c * 8 + 1) * BLOCK, 7 * (BLOCK - GROUP), slot_recv.at[c])
+        for j in (2, 1, 3):
+            at = pl.ds((c * 3 + j - 1) * LANES, LANES)
+            partial_out[at, :] = collect(c, j)
+            remote(
+                partial_out.at[at], partial_in.at[at],
+                partial_send, partial_recv.at[c], device({AXES[c % 3][2]: j}, 0),
+            )
+        if c < EARLY:
+            send_slots(c, 0, GROUP, own_recv)
+    for c in range(EARLY, UNITS):
+        send_slots(c, 0, GROUP, own_recv)
+    for c in range(UNITS):
+        whole(slots_in, (c * 8 + 1) * BLOCK, 7 * GROUP, own_recv.at[c])
+        own_sum[pl.ds(c * LANES, LANES), :] = collect(c, 0)
     for c in range(UNITS):
         whole(partial_in, c * 3 * LANES, 3 * LANES, partial_recv.at[c])
         total = own_sum[pl.ds(c * LANES, LANES), :]
         for j in range(3):
             total += partial_in[pl.ds((c * 3 + j) * LANES, LANES), :]
         regroup[pl.ds(c, LANES, stride=PITCH), :] = total
-    loads[4].wait()
+    loads[6].wait()
     for xo in range(tile_rows):
         parts = [
             regroup[pl.ds((xo * tile_cols + yo) * PITCH, UNITS), :] for yo in range(tile_cols)
@@ -454,7 +457,7 @@
                 remote(ymsg, yall.at[q], y_send, y_recv, device({2: dz, 0: dx}, 0))
     yall[q] = y_ends
 
-    loads[5].wait()
+    loads[7].wait()
     for z in range(planes):
         value = smooth[z] + (
             xfill[z] * flow[z : z + 1] + xfill[planes + z] * flow[planes + z : planes + z + 1]
@@ -476,6 +479,17 @@
     whole(yall, 0, n_gy - 1, y_send)
 
 
+def store(pushed_ref, next_ref, pushed_out, next_out, sems):
+    copies = [
+        pltpu.make_async_copy(pushed_ref, pushed_out, sems.at[0]),
+        pltpu.make_async_copy(next_ref, next_out, sems.at[1]),
+    ]
+    for copy in copies:
+        copy.start()
+    for copy in copies:
+        copy.wait()
+
+
 def per_device(source_mass, target_density, potential, dest_device, dest_tile, mass_counts, reach):
     planes, cx, cy = source_mass.shape
 
@@ -491,7 +505,7 @@
     def rows(count):
         return vmem((count, LANES), F32)
 
-    return pl.pallas_call(
+    fields = pl.pallas_call(
         kernel,
         out_shape=(grid, grid),
         in_specs=[hbm] * 7,
@@ -524,8 +538,8 @@
             vmem((8, 8, cy), F32),
             vmem((8, cx), F32),
             vmem((16, 8, cx), F32),
-            dma((7,)), dma, dma((3,)), dma, dma((UNITS,)),
-            dma, dma((UNITS,)), dma, dma((3,)), dma, dma((UNITS,)),
+            dma((8,)), dma, dma((3,)), dma, dma((UNITS,)),
+            dma, dma((UNITS,)), dma((UNITS,)), dma, dma((3,)), dma, dma((UNITS,)),
             dma, dma, dma, dma,
         ],
         compiler_params=pltpu.CompilerParams(collective_id=0, has_side_effects=True, vmem_limit_bytes=40 * 1024 * 1024),
@@ -539,6 +553,17 @@
             )
         ],
     )
+
+    local = pl.BlockSpec(memory_space=vmem)
+    return pl.pallas_call(
+        store,
+        out_shape=(grid, grid),
+        in_specs=[local, local],
+        out_specs=(hbm, hbm),
+        scratch_shapes=[dma((2,))],
+        compiler_params=pltpu.CompilerParams(vmem_limit_bytes=4 * 1024 * 1024),
+        name="store",
+    )(*fields)
 
 
 def solution(mesh):

time: 50 us -> 49.1 us (0.982)
  local copies, waits for them, and re-layouts: 1.59 us -> 0 us
  Pallas kernels: 47.3 us -> 48.3 us
    unnamed x2 -> x0, local copies, waits for them, and re-layouts: 1.59 us -> none
    pallas_call x0 -> x1, Pallas kernels: none -> 0.99 us  [per_device(): pl.pallas_call(store, out_shape=(grid, grid), in_specs=[local, local], ou...]
where the time goes in v5:
time: 49.1 us; the launch traced here: 49 us
  Pallas kernels  48.3 us (98%)
  between operations  0.64 us (1%)
    pallas_call x1, Pallas kernels, per_device(): pl.pallas_call(kernel, out_shape=(grid, grid), in_specs=[hbm] * 7, out_sp...  47.3 us
    pallas_call x1, Pallas kernels, per_device(): pl.pallas_call(store, out_shape=(grid, grid), in_specs=[local, local], ou...  0.99 us

profile of v5, /device:TPU:0, one launch (start us, length us, event | category | flops | bytes accessed | tf_op | source)
XLA Modules:
  0.0 49.0 jit_solution(5592323748432121465)
XLA Ops:
  0.6 47.3 %dual_step.1 = (f32[4,256,128]{2,1,0:T(8,128)S(1)}, f32[4,256,128]{2,1,0:T(8,128)S(1)}) custom-call(f32[4,256,128]{2,1,0:T(8,128)} %source_ref.1, f32[4,256,128]{2,1,0:T(8,128)} %target_ref.1, f32[4,256,128]{2,1,0:T(8,128)} %potential_ref.1, s32[4,128]{1,0:T(4,128)} %bitcast.9, s32[4,128]{1,0:T(4,128)} %bitcast.10, s32[4,128]{1,0:T(4,128)} %bitcast.11, ...), custom_call_target="tpu_custom_call" | custom-call | tf_op jit(solution)/shard_map/dual_step/pallas_call | solution.py:508
  48.0 1.0 %store.1 = (f32[4,256,128]{2,1,0:T(8,128)}, f32[4,256,128]{2,1,0:T(8,128)}) custom-call(f32[4,256,128]{2,1,0:T(8,128)S(1)} %get-tuple-element.4.pushed_ref, f32[4,256,128]{2,1,0:T(8,128)S(1)} %get-tuple-element.5.next_ref), custom_call_target="tpu_custom_call" | custom-call | tf_op jit(solution)/shard_map/store/pallas_call | solution.py:558

commit v6 on v5

--- a/solution.py
+++ b/solution.py
@@ -13,7 +13,6 @@
 AXES = ((0, 1, 2), (1, 2, 0), (2, 0, 1))
 GROUP = SLOTS * 4
 BLOCK = 4 * GROUP
-EARLY = 5
 PITCH = 9
 F32 = jnp.float32
 BF16 = jnp.bfloat16
@@ -76,17 +75,18 @@
     natural, target, potential, smooth, reach_ref,
     meta, metas, tiles, regroup, spread_in, picks, weights, places,
     slots_out, slots_in, labels_out, labels_in,
-    partial_out, partial_in, own_sum,
+    far_out, far_in, partial_out, partial_in, own_sum,
     xtab_hi, xtab_lo, ytab_hi, ytab_lo, xends_tab, yends_tab, xfill, yfill_tab,
     coef, edge_rows, halves, xmsg, xall, ymsg, yall,
     load_sem, meta_send, meta_recv, spread_send, spread_recv,
-    slot_send, slot_recv, own_recv, label_send, label_recv,
+    slot_send, slot_recv, own_recv, label_send, label_recv, far_send, far_recv,
     partial_send, partial_recv, x_send, x_recv, y_send, y_recv,
 ):
     p, q = lax.axis_index("gx"), lax.axis_index("gy")
     n_gx, n_gy = 8, 16
     planes, cx, cy = source_ref.shape
     tile_rows, tile_cols = cx // TS, cy // TS
+    half = LANES // 2
     here = (q & 3, p >> 1, q >> 2)
     core = p & 1
     stride = (1, 2 * n_gy, 4)
@@ -393,28 +393,49 @@
         value = dot(selects[c % 3][j], jnp.concatenate(split2(rows), axis=1))
         return value[:, :LANES] + value[:, LANES:]
 
+    def partial_row(c, s):
+        return (c * 2 + s) * LANES
+
+    sides = ((0, 1), (1, 3))
+
+    def send_partial(c, s, move, r):
+        at = pl.ds(partial_row(c, s) + r * half, half)
+        remote(
+            partial_out.at[at], partial_in.at[at],
+            partial_send, partial_recv.at[c], device({AXES[c % 3][2]: move}, 0),
+        )
+
     for c in range(UNITS):
         whole(slots_in, (c * 8 + 1) * BLOCK, 7 * (BLOCK - GROUP), slot_recv.at[c])
-        for j in (2, 1, 3):
-            at = pl.ds((c * 3 + j - 1) * LANES, LANES)
-            partial_out[at, :] = collect(c, j)
+        far_out[pl.ds(c * LANES, LANES), :] = collect(c, 2)
+        for s, move in sides:
+            at = pl.ds(c * LANES + s * half, half)
             remote(
-                partial_out.at[at], partial_in.at[at],
-                partial_send, partial_recv.at[c], device({AXES[c % 3][2]: j}, 0),
-            )
-        if c < EARLY:
-            send_slots(c, 0, GROUP, own_recv)
-    for c in range(EARLY, UNITS):
+                far_out.at[at], far_in.at[at],
+                far_send, far_recv.at[c], device({AXES[c % 3][2]: move}, 0),
+            )
+        for s, move in sides:
+            partial_out[pl.ds(partial_row(c, s), LANES), :] = collect(c, move)
+            send_partial(c, s, move, 1 - s)
         send_slots(c, 0, GROUP, own_recv)
+    for c in range(UNITS):
+        whole(far_in, c * LANES, LANES, far_recv.at[c])
+        for s, move in sides:
+            at = pl.ds(partial_row(c, s) + s * half, half)
+            partial_out[at, :] = (
+                partial_out[at, :] + far_in[pl.ds(c * LANES + s * half, half), :]
+            )
+            send_partial(c, s, move, s)
     for c in range(UNITS):
         whole(slots_in, (c * 8 + 1) * BLOCK, 7 * GROUP, own_recv.at[c])
         own_sum[pl.ds(c * LANES, LANES), :] = collect(c, 0)
     for c in range(UNITS):
-        whole(partial_in, c * 3 * LANES, 3 * LANES, partial_recv.at[c])
-        total = own_sum[pl.ds(c * LANES, LANES), :]
-        for j in range(3):
-            total += partial_in[pl.ds((c * 3 + j) * LANES, LANES), :]
-        regroup[pl.ds(c, LANES, stride=PITCH), :] = total
+        whole(partial_in, partial_row(c, 0), 2 * LANES, partial_recv.at[c])
+        regroup[pl.ds(c, LANES, stride=PITCH), :] = (
+            own_sum[pl.ds(c * LANES, LANES), :]
+            + partial_in[pl.ds(partial_row(c, 0), LANES), :]
+            + partial_in[pl.ds(partial_row(c, 1), LANES), :]
+        )
     loads[6].wait()
     for xo in range(tile_rows):
         parts = [
@@ -474,7 +495,8 @@
     whole(spread_in, 0, 3 * UNITS * LANES, spread_send)
     whole(slots_out, 0, 7 * UNITS * BLOCK, slot_send)
     whole(labels_out, 0, 21, label_send)
-    whole(partial_out, 0, 3 * UNITS * LANES, partial_send)
+    whole(far_out, 0, UNITS * LANES, far_send)
+    whole(partial_out, 0, 2 * UNITS * LANES, partial_send)
     whole(xall, 0, n_gx - 1, x_send)
     whole(yall, 0, n_gy - 1, y_send)
 
@@ -522,7 +544,8 @@
             rows(7 * UNITS * BLOCK + 8), rows(8 * UNITS * BLOCK + 8),
             vmem((24, 1, LANES), F32),
             vmem((24, 1, LANES), F32),
-            rows(3 * UNITS * LANES), rows(3 * UNITS * LANES), rows(UNITS * LANES),
+            rows(UNITS * LANES), rows(UNITS * LANES),
+            rows(2 * UNITS * LANES), rows(2 * UNITS * LANES), rows(UNITS * LANES),
             vmem((planes, cx, cx), BF16),
             vmem((planes, cx, cx), BF16),
             vmem((planes, cy, cy), BF16),
@@ -540,6 +563,7 @@
             vmem((16, 8, cx), F32),
             dma((8,)), dma, dma((3,)), dma, dma((UNITS,)),
             dma, dma((UNITS,)), dma((UNITS,)), dma, dma((3,)), dma, dma((UNITS,)),
+            dma, dma((UNITS,)),
             dma, dma, dma, dma,
         ],
         compiler_params=pltpu.CompilerParams(collective_id=0, has_side_effects=True, vmem_limit_bytes=40 * 1024 * 1024),

time: 49.1 us -> 48.3 us (0.984)
  Pallas kernels: 48.3 us -> 47.1 us
    pallas_call x1, Pallas kernels: 47.3 us -> 46.1 us  [per_device(): pl.pallas_call(kernel, out_shape=(grid, grid), in_specs=[hbm] * 7, out_sp...]
where the time goes in v6:
time: 48.3 us; the launch traced here: 47.7 us
  Pallas kernels  47.1 us (98%)
  between operations  0.64 us (1%)
    pallas_call x1, Pallas kernels, per_device(): pl.pallas_call(kernel, out_shape=(grid, grid), in_specs=[hbm] * 7, out_sp...  46.1 us
    pallas_call x1, Pallas kernels, per_device(): pl.pallas_call(store, out_shape=(grid, grid), in_specs=[local, local], ou...  0.99 us

profile of v6, /device:TPU:0, one launch (start us, length us, event | category | flops | bytes accessed | tf_op | source)
XLA Modules:
  0.0 47.7 jit_solution(12630706977220896086)
XLA Ops:
  0.6 46.1 %dual_step.1 = (f32[4,256,128]{2,1,0:T(8,128)S(1)}, f32[4,256,128]{2,1,0:T(8,128)S(1)}) custom-call(f32[4,256,128]{2,1,0:T(8,128)} %source_ref.1, f32[4,256,128]{2,1,0:T(8,128)} %target_ref.1, f32[4,256,128]{2,1,0:T(8,128)} %potential_ref.1, s32[4,128]{1,0:T(4,128)} %bitcast.9, s32[4,128]{1,0:T(4,128)} %bitcast.10, s32[4,128]{1,0:T(4,128)} %bitcast.11, ...), custom_call_target="tpu_custom_call" | custom-call | tf_op jit(solution)/shard_map/dual_step/pallas_call | solution.py:530
  46.7 1.0 %store.1 = (f32[4,256,128]{2,1,0:T(8,128)}, f32[4,256,128]{2,1,0:T(8,128)}) custom-call(f32[4,256,128]{2,1,0:T(8,128)S(1)} %get-tuple-element.4.pushed_ref, f32[4,256,128]{2,1,0:T(8,128)S(1)} %get-tuple-element.5.next_ref), custom_call_target="tpu_custom_call" | custom-call | tf_op jit(solution)/shard_map/store/pallas_call | solution.py:582

commit v7 on v6

--- a/solution.py
+++ b/solution.py
@@ -13,6 +13,7 @@
 AXES = ((0, 1, 2), (1, 2, 0), (2, 0, 1))
 GROUP = SLOTS * 4
 BLOCK = 4 * GROUP
+EARLY = 5
 PITCH = 9
 F32 = jnp.float32
 BF16 = jnp.bfloat16
@@ -21,6 +22,13 @@
 def split2(a):
     hi = a.astype(BF16)
     return hi, (a - hi.astype(F32)).astype(BF16)
+
+
+def split3(a):
+    hi = a.astype(BF16)
+    rest = a - hi.astype(F32)
+    mid = rest.astype(BF16)
+    return hi, mid, (rest - mid.astype(F32)).astype(BF16)
 
 
 def dot(a, b, dims=((1,), (0,))):
@@ -77,7 +85,7 @@
     slots_out, slots_in, labels_out, labels_in,
     far_out, far_in, partial_out, partial_in, own_sum,
     xtab_hi, xtab_lo, ytab_hi, ytab_lo, xends_tab, yends_tab, xfill, yfill_tab,
-    coef, edge_rows, halves, xmsg, xall, ymsg, yall,
+    coef, edge_rows, column_tab, halves, xmsg, xall, ymsg, yall,
     load_sem, meta_send, meta_recv, spread_send, spread_recv,
     slot_send, slot_recv, own_recv, label_send, label_recv, far_send, far_recv,
     partial_send, partial_recv, x_send, x_recv, y_send, y_recv,
@@ -182,14 +190,16 @@
     sums_x, last_x, first_x, swept_x, fall_x = rows_of(cx)
     sums_y, last_rows, first_rows, swept_y, fall_y = rows_of(cy)
     edge_rows[0], edge_rows[1] = swept_x, fall_x
-    spare = jnp.zeros((cy - 24, cx), F32)
-    columns = jnp.transpose(
+    spare = jnp.zeros((cy - 32, cx), F32)
+    column_tab[...] = jnp.transpose(
         jnp.concatenate(
             [sums_x, jnp.where(upper, swept_x, fall_x),
-             jnp.concatenate([sums_y, sums_y], axis=1), spare],
+             jnp.concatenate([sums_y, sums_y], axis=1),
+             jnp.where(upper, last_x, first_x), spare],
             axis=0,
         )
     )
+    columns = column_tab[...]
     across_row = iota((cy, cy), 0)
     gap = across_row - iota((cy, cy), 1)
     for z in range(planes):
@@ -385,6 +395,27 @@
             row_of.append((tile_index == named).astype(BF16))
         selects.append(row_of)
 
+    part_lane = iota((LANES, LANES), 1)
+    source_lane = iota((LANES, LANES), 0)
+    unit_row = iota((LANES, cx), 0)
+    cell = iota((LANES, cx), 1)
+    unit_weights = []
+    for first in (24, 24 + planes):
+        expand = (source_lane == first + (part_lane >> 5)).astype(BF16)
+        values = sum(dot(part, expand) for part in split3(column_tab[...]))
+        values = split3(values)
+        rows = []
+        for h in range(2):
+            pick = (cell == (unit_row & 15) * TS + h * 8 + (unit_row >> 4)).astype(BF16)
+            rows.append(sum(dot(pick, part) for part in values))
+        unit_weights.append(jnp.where((part_lane & TS) == 0, rows[0], rows[1]))
+    loads[6].wait()
+    ends = jnp.zeros((8, cy), F32)
+    for z in range(planes):
+        value = dot(xends_tab[z], jnp.concatenate(split2(target[z]), axis=1))
+        ends += value[:8, :cy] + (value[:8, cy:] + value[8:, :cy])
+    unit_ends = [jnp.zeros((8, LANES), F32), jnp.zeros((8, LANES), F32)]
+
     def collect(c, j):
         rows = jnp.concatenate(
             [slots_in[pl.ds((c * 8 + ih) * BLOCK + j * GROUP, GROUP), :] for ih in range(8)],
@@ -417,8 +448,12 @@
         for s, move in sides:
             partial_out[pl.ds(partial_row(c, s), LANES), :] = collect(c, move)
             send_partial(c, s, move, 1 - s)
-        send_slots(c, 0, GROUP, own_recv)
+        if c < EARLY:
+            send_slots(c, 0, GROUP, own_recv)
     for c in range(UNITS):
+        if c == EARLY:
+            for last in range(EARLY, UNITS):
+                send_slots(last, 0, GROUP, own_recv)
         whole(far_in, c * LANES, LANES, far_recv.at[c])
         for s, move in sides:
             at = pl.ds(partial_row(c, s) + s * half, half)
@@ -431,31 +466,44 @@
         own_sum[pl.ds(c * LANES, LANES), :] = collect(c, 0)
     for c in range(UNITS):
         whole(partial_in, partial_row(c, 0), 2 * LANES, partial_recv.at[c])
-        regroup[pl.ds(c, LANES, stride=PITCH), :] = (
+        total = (
             own_sum[pl.ds(c * LANES, LANES), :]
             + partial_in[pl.ds(partial_row(c, 0), LANES), :]
             + partial_in[pl.ds(partial_row(c, 1), LANES), :]
         )
-    loads[6].wait()
+        for i in range(2):
+            terms = [
+                total[xo * 8 : (xo + 1) * 8] * unit_weights[i][c * 16 + xo : c * 16 + xo + 1]
+                for xo in range(tile_rows)
+            ]
+            while len(terms) > 1:
+                terms = [a + b for a, b in zip(terms[::2], terms[1::2])]
+            unit_ends[i] = unit_ends[i] + terms[0]
+        regroup[pl.ds(c, LANES, stride=PITCH), :] = total
+
+    lane = iota((8, LANES), 1)
+    last, first = [a + pltpu.roll(a, LANES - TS, 1) for a in unit_ends]
+    block = lane >> 4 == iota((8, LANES), 0)
+    for i, value in enumerate((last, first)):
+        for z in range(planes):
+            moved = pltpu.roll(value, (LANES - 2 * TS * z) % LANES, 1) if z else value
+            moved = pltpu.roll(moved, 0, 1, stride=TS, stride_axis=0)
+            moved = jnp.sum(jnp.where(block, moved, 0.0), axis=0, keepdims=True)
+            ends -= jnp.where(row8 == i * planes + z, moved, 0.0)
+    xmsg[...] = ends
+    for s in range(4):
+        for h in range(2):
+            if s + h:
+                remote(xmsg, xall.at[p], x_send, x_recv, device({1: s}, h))
+    xall[p] = ends
     for xo in range(tile_rows):
         parts = [
             regroup[pl.ds((xo * tile_cols + yo) * PITCH, UNITS), :] for yo in range(tile_cols)
         ]
         for g, value in enumerate(block_transpose(parts)):
             pushed_ref[g // 2, pl.ds(xo * TS + (g % 2) * 8, 8), :] = value
-
-    ends = jnp.zeros((8, cy), F32)
     for z in range(planes):
-        both = jnp.concatenate(split2(target[z] - pushed_ref[z]), axis=1)
-        halves[z] = both
-        value = dot(xends_tab[z], both)
-        ends += value[:8, :cy] + (value[:8, cy:] + value[8:, :cy])
-    xmsg[...] = ends
-    for s in range(4):
-        for h in range(2):
-            if s + h:
-                remote(xmsg, xall.at[p], x_send, x_recv, device({1: s}, h))
-    xall[p] = ends
+        halves[z] = jnp.concatenate(split2(target[z] - pushed_ref[z]), axis=1)
     y_ends = jnp.zeros((8, cx), F32)
     for z in range(planes):
         both = halves[z]
@@ -556,6 +604,7 @@
             vmem((planes, 32, cy), BF16),
             vmem((48, 8, LANES), F32),
             vmem((2, 8, cx), F32),
+            vmem((cx, LANES), F32),
             vmem((planes, cx, 2 * cy), BF16),
             vmem((8, cy), F32),
             vmem((8, 8, cy), F32),

time: 48.3 us -> 47.6 us (0.986)
  no operation moved by 1% of the time
where the time goes in v7:
time: 47.6 us; the launch traced here: 47.3 us
  Pallas kernels  46.7 us (98%)
  between operations  0.64 us (1%)
    pallas_call x1, Pallas kernels, per_device(): pl.pallas_call(kernel, out_shape=(grid, grid), in_specs=[hbm] * 7, out_sp...  45.7 us
    pallas_call x1, Pallas kernels, per_device(): pl.pallas_call(store, out_shape=(grid, grid), in_specs=[local, local], ou...  0.99 us

profile of v7, /device:TPU:0, one launch (start us, length us, event | category | flops | bytes accessed | tf_op | source)
XLA Modules:
  0.0 47.3 jit_solution(5818010224317707996)
XLA Ops:
  0.6 45.7 %dual_step.1 = (f32[4,256,128]{2,1,0:T(8,128)S(1)}, f32[4,256,128]{2,1,0:T(8,128)S(1)}) custom-call(f32[4,256,128]{2,1,0:T(8,128)} %source_ref.1, f32[4,256,128]{2,1,0:T(8,128)} %target_ref.1, f32[4,256,128]{2,1,0:T(8,128)} %potential_ref.1, s32[4,128]{1,0:T(4,128)} %bitcast.9, s32[4,128]{1,0:T(4,128)} %bitcast.10, s32[4,128]{1,0:T(4,128)} %bitcast.11, ...), custom_call_target="tpu_custom_call" | custom-call | tf_op jit(solution)/shard_map/dual_step/pallas_call | solution.py:578
  46.4 1.0 %store.1 = (f32[4,256,128]{2,1,0:T(8,128)}, f32[4,256,128]{2,1,0:T(8,128)}) custom-call(f32[4,256,128]{2,1,0:T(8,128)S(1)} %get-tuple-element.4.pushed_ref, f32[4,256,128]{2,1,0:T(8,128)S(1)} %get-tuple-element.5.next_ref), custom_call_target="tpu_custom_call" | custom-call | tf_op jit(solution)/shard_map/store/pallas_call | solution.py:631

commit v8 on v7

--- a/solution.py
+++ b/solution.py
@@ -13,7 +13,6 @@
 AXES = ((0, 1, 2), (1, 2, 0), (2, 0, 1))
 GROUP = SLOTS * 4
 BLOCK = 4 * GROUP
-EARLY = 5
 PITCH = 9
 F32 = jnp.float32
 BF16 = jnp.bfloat16
@@ -85,10 +84,10 @@
     slots_out, slots_in, labels_out, labels_in,
     far_out, far_in, partial_out, partial_in, own_sum,
     xtab_hi, xtab_lo, ytab_hi, ytab_lo, xends_tab, yends_tab, xfill, yfill_tab,
-    coef, edge_rows, column_tab, halves, xmsg, xall, ymsg, yall,
+    coef, edge_rows, column_tab, halves, corner_coef, corner_out, corners, xmsg, xall, ymsg, yall,
     load_sem, meta_send, meta_recv, spread_send, spread_recv,
     slot_send, slot_recv, own_recv, label_send, label_recv, far_send, far_recv,
-    partial_send, partial_recv, x_send, x_recv, y_send, y_recv,
+    partial_send, partial_recv, x_send, x_recv, y_send, y_recv, corner_send, corner_recv,
 ):
     p, q = lax.axis_index("gx"), lax.axis_index("gy")
     n_gx, n_gy = 8, 16
@@ -360,6 +359,13 @@
     for c in range(UNITS):
         pack(c)
 
+    corner_lane = iota((8, LANES), 1)
+    corner_row = (corner_lane >> 3) * planes + (corner_lane & 3) == iota((8, LANES), 0)
+    for i in range(2 * n_gx):
+        corner_coef[pl.ds(i, 1), :] = jnp.sum(
+            jnp.where(corner_row, coef[i], 0.0), axis=0, keepdims=True
+        )
+
     def inflow(base, count, all_ref, width):
         columns = []
         for w in range(width // LANES):
@@ -448,12 +454,8 @@
         for s, move in sides:
             partial_out[pl.ds(partial_row(c, s), LANES), :] = collect(c, move)
             send_partial(c, s, move, 1 - s)
-        if c < EARLY:
-            send_slots(c, 0, GROUP, own_recv)
+        send_slots(c, 0, GROUP, own_recv)
     for c in range(UNITS):
-        if c == EARLY:
-            for last in range(EARLY, UNITS):
-                send_slots(last, 0, GROUP, own_recv)
         whole(far_in, c * LANES, LANES, far_recv.at[c])
         for s, move in sides:
             at = pl.ds(partial_row(c, s) + s * half, half)
@@ -496,6 +498,24 @@
             if s + h:
                 remote(xmsg, xall.at[p], x_send, x_recv, device({1: s}, h))
     xall[p] = ends
+    at_last = jnp.sum(ends * last_rows, axis=1, keepdims=True)
+    at_first = jnp.sum(ends * first_rows, axis=1, keepdims=True)
+    corner = jnp.sum(
+        jnp.where(corner_row, jnp.where((corner_lane & 4) == 0, at_last, at_first), 0.0),
+        axis=0, keepdims=True,
+    )
+    here_block = p * n_gy + q
+    corner_out[0] = corner
+    corners[here_block] = corner
+    for far in (2, 1, 3, 0):
+        for dz in (2, 1, 3, 0):
+            for dx in (2, 1, 3, 0):
+                for h in range(2):
+                    if far + h + dz + dx:
+                        remote(
+                            corner_out.at[0], corners.at[here_block], corner_send, corner_recv,
+                            device({1: far, 2: dz, 0: dx}, h),
+                        )
     for xo in range(tile_rows):
         parts = [
             regroup[pl.ds((xo * tile_cols + yo) * PITCH, UNITS), :] for yo in range(tile_cols)
@@ -512,19 +532,14 @@
         smooth[z] = value
         value = dot(yends_tab[z], jnp.concatenate(split2(value), axis=0), ((1,), (1,)))
         y_ends += value[:8, :cx] + (value[:8, cx:] + value[8:, :cx])
-    whole(xall, 0, n_gx - 1, x_recv)
-    flow = inflow(0, n_gx, xall, cy)
-    at_last = jnp.sum(flow * last_rows, axis=1, keepdims=True)
-    at_first = jnp.sum(flow * first_rows, axis=1, keepdims=True)
-    entered = jnp.where(upper, at_last, pltpu.roll(jnp.broadcast_to(at_first, (8, LANES)), 4, 0)[:, 0:1])
-    left = jnp.where(upper, pltpu.roll(jnp.broadcast_to(at_last, (8, LANES)), 4, 0)[:, 0:1], at_first)
-    y_ends += edge_rows[0] * entered + edge_rows[1] * left
     ymsg[...] = y_ends
     for dz in range(4):
         for dx in range(4):
             if dz + dx:
                 remote(ymsg, yall.at[q], y_send, y_recv, device({2: dz, 0: dx}, 0))
     yall[q] = y_ends
+    whole(xall, 0, n_gx - 1, x_recv)
+    flow = inflow(0, n_gx, xall, cy)
 
     loads[7].wait()
     for z in range(planes):
@@ -532,7 +547,26 @@
             xfill[z] * flow[z : z + 1] + xfill[planes + z] * flow[planes + z : planes + z + 1]
         )
         potential[z] = potential[z] + dot3(split2(value), (ytab_hi[z], ytab_lo[z]))
+    whole(corners, 0, n_gx * n_gy - 1, corner_recv)
+    direct, through = [], []
+    for i in range(n_gx):
+        value = corners[pl.ds(i * n_gy, n_gy)].reshape(n_gy, LANES)
+        direct.append(value * corner_coef[pl.ds(i, 1), :])
+        through.append(value * corner_coef[pl.ds(n_gx + i, 1), :])
+    while len(direct) > 1:
+        direct = [a + b for a, b in zip(direct[::2], direct[1::2])]
+        through = [a + b for a, b in zip(through[::2], through[1::2])]
+    crossed = direct[0] + pltpu.roll(through[0], 8, 1)
+    crossed = jnp.transpose(
+        jnp.concatenate([crossed, jnp.zeros((LANES - n_gy, LANES), F32)], axis=0)
+    )
     whole(yall, 0, n_gy - 1, y_recv)
+    for i in range(n_gy):
+        yall[i] = (
+            yall[i]
+            + edge_rows[0] * crossed[0:8, i : i + 1]
+            + edge_rows[1] * crossed[8:16, i : i + 1]
+        )
     flow = inflow(2 * n_gx, n_gy, yall, cx)
     hi = flow.astype(BF16).astype(F32)
     flow = jnp.concatenate([hi, flow - hi, hi, flow - hi], axis=0).astype(BF16)
@@ -547,6 +581,7 @@
     whole(partial_out, 0, 2 * UNITS * LANES, partial_send)
     whole(xall, 0, n_gx - 1, x_send)
     whole(yall, 0, n_gy - 1, y_send)
+    whole(corners, 0, n_gx * n_gy - 1, corner_send)
 
 
 def store(pushed_ref, next_ref, pushed_out, next_out, sems):
@@ -606,6 +641,9 @@
             vmem((2, 8, cx), F32),
             vmem((cx, LANES), F32),
             vmem((planes, cx, 2 * cy), BF16),
+            vmem((16, LANES), F32),
+            vmem((1, 1, LANES), F32),
+            vmem((LANES, 1, LANES), F32),
             vmem((8, cy), F32),
             vmem((8, 8, cy), F32),
             vmem((8, cx), F32),
@@ -613,7 +651,7 @@
             dma((8,)), dma, dma((3,)), dma, dma((UNITS,)),
             dma, dma((UNITS,)), dma((UNITS,)), dma, dma((3,)), dma, dma((UNITS,)),
             dma, dma((UNITS,)),
-            dma, dma, dma, dma,
+            dma, dma, dma, dma, dma, dma,
         ],
         compiler_params=pltpu.CompilerParams(collective_id=0, has_side_effects=True, vmem_limit_bytes=40 * 1024 * 1024),
         name="dual_step",

time: 47.6 us -> 45.9 us (0.964)
  Pallas kernels: 46.7 us -> 45.1 us
    pallas_call x1, Pallas kernels: 45.7 us -> 44.1 us  [per_device(): pl.pallas_call(kernel, out_shape=(grid, grid), in_specs=[hbm] * 7, out_sp...]
where the time goes in v8:
time: 45.9 us; the launch traced here: 45.8 us
  Pallas kernels  45.1 us (98%)
  between operations  0.64 us (1%)
    pallas_call x1, Pallas kernels, per_device(): pl.pallas_call(kernel, out_shape=(grid, grid), in_specs=[hbm] * 7, out_sp...  44.1 us
    pallas_call x1, Pallas kernels, per_device(): pl.pallas_call(store, out_shape=(grid, grid), in_specs=[local, local], ou...  0.99 us

profile of v8, /device:TPU:0, one launch (start us, length us, event | category | flops | bytes accessed | tf_op | source)
XLA Modules:
  0.0 45.8 jit_solution(11937578913773243571)
XLA Ops:
  0.6 44.1 %dual_step.1 = (f32[4,256,128]{2,1,0:T(8,128)S(1)}, f32[4,256,128]{2,1,0:T(8,128)S(1)}) custom-call(f32[4,256,128]{2,1,0:T(8,128)} %source_ref.1, f32[4,256,128]{2,1,0:T(8,128)} %target_ref.1, f32[4,256,128]{2,1,0:T(8,128)} %potential_ref.1, s32[4,128]{1,0:T(4,128)} %bitcast.9, s32[4,128]{1,0:T(4,128)} %bitcast.10, s32[4,128]{1,0:T(4,128)} %bitcast.11, ...), custom_call_target="tpu_custom_call" | custom-call | tf_op jit(solution)/shard_map/dual_step/pallas_call | solution.py:613
  44.8 1.0 %store.1 = (f32[4,256,128]{2,1,0:T(8,128)}, f32[4,256,128]{2,1,0:T(8,128)}) custom-call(f32[4,256,128]{2,1,0:T(8,128)S(1)} %get-tuple-element.4.pushed_ref, f32[4,256,128]{2,1,0:T(8,128)S(1)} %get-tuple-element.5.next_ref), custom_call_target="tpu_custom_call" | custom-call | tf_op jit(solution)/shard_map/store/pallas_call | solution.py:669

commit v9 on v8

--- a/solution.py
+++ b/solution.py
@@ -84,7 +84,7 @@
     slots_out, slots_in, labels_out, labels_in,
     far_out, far_in, partial_out, partial_in, own_sum,
     xtab_hi, xtab_lo, ytab_hi, ytab_lo, xends_tab, yends_tab, xfill, yfill_tab,
-    coef, edge_rows, column_tab, halves, corner_coef, corner_out, corners, xmsg, xall, ymsg, yall,
+    coef, edge_rows, column_tab, halves, line_coef, corner_coef, corner_out, corners, xmsg, xall, ymsg, yall,
     load_sem, meta_send, meta_recv, spread_send, spread_recv,
     slot_send, slot_recv, own_recv, label_send, label_recv, far_send, far_recv,
     partial_send, partial_recv, x_send, x_recv, y_send, y_recv, corner_send, corner_recv,
@@ -366,6 +366,12 @@
             jnp.where(corner_row, coef[i], 0.0), axis=0, keepdims=True
         )
 
+    for k in range(2):
+        value = jnp.zeros((8, LANES), F32)
+        for i in range(n_gy):
+            value = jnp.where(corner_lane == i, coef[2 * n_gx + k * n_gy + i], value)
+        line_coef[k] = value
+
     def inflow(base, count, all_ref, width):
         columns = []
         for w in range(width // LANES):
@@ -507,15 +513,21 @@
     here_block = p * n_gy + q
     corner_out[0] = corner
     corners[here_block] = corner
-    for far in (2, 1, 3, 0):
-        for dz in (2, 1, 3, 0):
-            for dx in (2, 1, 3, 0):
-                for h in range(2):
-                    if far + h + dz + dx:
-                        remote(
-                            corner_out.at[0], corners.at[here_block], corner_send, corner_recv,
-                            device({1: far, 2: dz, 0: dx}, h),
-                        )
+    moves = [
+        (sum(min(v, 4 - v) for v in (dx, dy, dz)), dx, dy, dz, h)
+        for dx in range(4) for dy in range(4) for dz in range(4) for h in range(2)
+    ]
+    moves = sorted(moves, reverse=True)[:-1]
+
+    def send_corner(hops, dx, dy, dz, h):
+        remote(
+            corner_out.at[0], corners.at[here_block], corner_send, corner_recv,
+            device({0: dx, 1: dy, 2: dz}, h),
+        )
+
+    for move in moves:
+        if move[0] >= 4:
+            send_corner(*move)
     for xo in range(tile_rows):
         parts = [
             regroup[pl.ds((xo * tile_cols + yo) * PITCH, UNITS), :] for yo in range(tile_cols)
@@ -538,6 +550,9 @@
             if dz + dx:
                 remote(ymsg, yall.at[q], y_send, y_recv, device({2: dz, 0: dx}, 0))
     yall[q] = y_ends
+    for move in moves:
+        if move[0] < 4:
+            send_corner(*move)
     whole(xall, 0, n_gx - 1, x_recv)
     flow = inflow(0, n_gx, xall, cy)
 
@@ -560,14 +575,16 @@
     crossed = jnp.transpose(
         jnp.concatenate([crossed, jnp.zeros((LANES - n_gy, LANES), F32)], axis=0)
     )
+
+    def crossed_by(k):
+        entered = jnp.sum(crossed[0:8] * line_coef[k], axis=1, keepdims=True)
+        left = jnp.sum(crossed[8:16] * line_coef[k], axis=1, keepdims=True)
+        return edge_rows[0] * entered + edge_rows[1] * left
+
+    crossing, far_crossing = crossed_by(0), crossed_by(1)
     whole(yall, 0, n_gy - 1, y_recv)
-    for i in range(n_gy):
-        yall[i] = (
-            yall[i]
-            + edge_rows[0] * crossed[0:8, i : i + 1]
-            + edge_rows[1] * crossed[8:16, i : i + 1]
-        )
     flow = inflow(2 * n_gx, n_gy, yall, cx)
+    flow += crossing + pltpu.roll(far_crossing, planes, 0)
     hi = flow.astype(BF16).astype(F32)
     flow = jnp.concatenate([hi, flow - hi, hi, flow - hi], axis=0).astype(BF16)
     for z in range(planes):
@@ -641,6 +658,7 @@
             vmem((2, 8, cx), F32),
             vmem((cx, LANES), F32),
             vmem((planes, cx, 2 * cy), BF16),
+            vmem((2, 8, LANES), F32),
             vmem((16, LANES), F32),
             vmem((1, 1, LANES), F32),
             vmem((LANES, 1, LANES), F32),

time: 45.9 us -> 47.4 us (1.033); the launches traced: 45.8 us -> 46.6 us
  Pallas kernels: 45.1 us -> 45.9 us
    pallas_call x1, Pallas kernels: 44.1 us -> 44.9 us  [per_device(): pl.pallas_call(kernel, out_shape=(grid, grid), in_specs=[hbm] * 7, out_sp...]
where the time goes in v9:
time: 47.4 us; the launch traced here: 46.6 us
  Pallas kernels  45.9 us (97%)
  between operations  0.64 us (1%)
    pallas_call x1, Pallas kernels, per_device(): pl.pallas_call(kernel, out_shape=(grid, grid), in_specs=[hbm] * 7, out_sp...  44.9 us
    pallas_call x1, Pallas kernels, per_device(): pl.pallas_call(store, out_shape=(grid, grid), in_specs=[local, local], ou...  0.99 us

profile of v9, /device:TPU:0, one launch (start us, length us, event | category | flops | bytes accessed | tf_op | source)
XLA Modules:
  0.0 46.6 jit_solution(2565714305532690967)
XLA Ops:
  0.6 44.9 %dual_step.1 = (f32[4,256,128]{2,1,0:T(8,128)S(1)}, f32[4,256,128]{2,1,0:T(8,128)S(1)}) custom-call(f32[4,256,128]{2,1,0:T(8,128)} %source_ref.1, f32[4,256,128]{2,1,0:T(8,128)} %target_ref.1, f32[4,256,128]{2,1,0:T(8,128)} %potential_ref.1, s32[4,128]{1,0:T(4,128)} %bitcast.9, s32[4,128]{1,0:T(4,128)} %bitcast.10, s32[4,128]{1,0:T(4,128)} %bitcast.11, ...), custom_call_target="tpu_custom_call" | custom-call | tf_op jit(solution)/shard_map/dual_step/pallas_call | solution.py:630
  45.6 1.0 %store.1 = (f32[4,256,128]{2,1,0:T(8,128)}, f32[4,256,128]{2,1,0:T(8,128)}) custom-call(f32[4,256,128]{2,1,0:T(8,128)S(1)} %get-tuple-element.4.pushed_ref, f32[4,256,128]{2,1,0:T(8,128)S(1)} %get-tuple-element.5.next_ref), custom_call_target="tpu_custom_call" | custom-call | tf_op jit(solution)/shard_map/store/pallas_call | solution.py:687

commit v10 on v8

--- a/solution.py
+++ b/solution.py
@@ -84,7 +84,7 @@
     slots_out, slots_in, labels_out, labels_in,
     far_out, far_in, partial_out, partial_in, own_sum,
     xtab_hi, xtab_lo, ytab_hi, ytab_lo, xends_tab, yends_tab, xfill, yfill_tab,
-    coef, edge_rows, column_tab, halves, corner_coef, corner_out, corners, xmsg, xall, ymsg, yall,
+    coef, edge_rows, column_tab, halves, line_coef, corner_coef, corner_out, corners, xmsg, xall, ymsg, yall,
     load_sem, meta_send, meta_recv, spread_send, spread_recv,
     slot_send, slot_recv, own_recv, label_send, label_recv, far_send, far_recv,
     partial_send, partial_recv, x_send, x_recv, y_send, y_recv, corner_send, corner_recv,
@@ -365,6 +365,12 @@
         corner_coef[pl.ds(i, 1), :] = jnp.sum(
             jnp.where(corner_row, coef[i], 0.0), axis=0, keepdims=True
         )
+
+    for k in range(2):
+        value = jnp.zeros((8, LANES), F32)
+        for i in range(n_gy):
+            value = jnp.where(corner_lane == i, coef[2 * n_gx + k * n_gy + i], value)
+        line_coef[k] = value
 
     def inflow(base, count, all_ref, width):
         columns = []
@@ -560,14 +566,16 @@
     crossed = jnp.transpose(
         jnp.concatenate([crossed, jnp.zeros((LANES - n_gy, LANES), F32)], axis=0)
     )
+
+    def crossed_by(k):
+        entered = jnp.sum(crossed[0:8] * line_coef[k], axis=1, keepdims=True)
+        left = jnp.sum(crossed[8:16] * line_coef[k], axis=1, keepdims=True)
+        return edge_rows[0] * entered + edge_rows[1] * left
+
+    crossing, far_crossing = crossed_by(0), crossed_by(1)
     whole(yall, 0, n_gy - 1, y_recv)
-    for i in range(n_gy):
-        yall[i] = (
-            yall[i]
-            + edge_rows[0] * crossed[0:8, i : i + 1]
-            + edge_rows[1] * crossed[8:16, i : i + 1]
-        )
     flow = inflow(2 * n_gx, n_gy, yall, cx)
+    flow += crossing + pltpu.roll(far_crossing, planes, 0)
     hi = flow.astype(BF16).astype(F32)
     flow = jnp.concatenate([hi, flow - hi, hi, flow - hi], axis=0).astype(BF16)
     for z in range(planes):
@@ -641,6 +649,7 @@
             vmem((2, 8, cx), F32),
             vmem((cx, LANES), F32),
             vmem((planes, cx, 2 * cy), BF16),
+            vmem((2, 8, LANES), F32),
             vmem((16, LANES), F32),
             vmem((1, 1, LANES), F32),
             vmem((LANES, 1, LANES), F32),

time: 45.9 us -> 45.8 us (level)
  no operation moved by 1% of the time
where the time goes in v10:
time: 45.8 us; the launch traced here: 45.7 us
  Pallas kernels  45 us (98%)
  between operations  0.64 us (1%)
    pallas_call x1, Pallas kernels, per_device(): pl.pallas_call(kernel, out_shape=(grid, grid), in_specs=[hbm] * 7, out_sp...  44 us
    pallas_call x1, Pallas kernels, per_device(): pl.pallas_call(store, out_shape=(grid, grid), in_specs=[local, local], ou...  0.99 us

profile of v10, /device:TPU:0, one launch (start us, length us, event | category | flops | bytes accessed | tf_op | source)
XLA Modules:
  0.0 45.7 jit_solution(16436801780714579351)
XLA Ops:
  0.6 44.0 %dual_step.1 = (f32[4,256,128]{2,1,0:T(8,128)S(1)}, f32[4,256,128]{2,1,0:T(8,128)S(1)}) custom-call(f32[4,256,128]{2,1,0:T(8,128)} %source_ref.1, f32[4,256,128]{2,1,0:T(8,128)} %target_ref.1, f32[4,256,128]{2,1,0:T(8,128)} %potential_ref.1, s32[4,128]{1,0:T(4,128)} %bitcast.9, s32[4,128]{1,0:T(4,128)} %bitcast.10, s32[4,128]{1,0:T(4,128)} %bitcast.11, ...), custom_call_target="tpu_custom_call" | custom-call | tf_op jit(solution)/shard_map/dual_step/pallas_call | solution.py:621
  44.7 1.0 %store.1 = (f32[4,256,128]{2,1,0:T(8,128)}, f32[4,256,128]{2,1,0:T(8,128)}) custom-call(f32[4,256,128]{2,1,0:T(8,128)S(1)} %get-tuple-element.4.pushed_ref, f32[4,256,128]{2,1,0:T(8,128)S(1)} %get-tuple-element.5.next_ref), custom_call_target="tpu_custom_call" | custom-call | tf_op jit(solution)/shard_map/store/pallas_call | solution.py:678

commit v11 on v10

--- a/solution.py
+++ b/solution.py
@@ -13,6 +13,7 @@
 AXES = ((0, 1, 2), (1, 2, 0), (2, 0, 1))
 GROUP = SLOTS * 4
 BLOCK = 4 * GROUP
+LAG = 3
 PITCH = 9
 F32 = jnp.float32
 BF16 = jnp.bfloat16
@@ -460,6 +461,9 @@
         for s, move in sides:
             partial_out[pl.ds(partial_row(c, s), LANES), :] = collect(c, move)
             send_partial(c, s, move, 1 - s)
+        if c >= LAG:
+            send_slots(c - LAG, 0, GROUP, own_recv)
+    for c in range(UNITS - LAG, UNITS):
         send_slots(c, 0, GROUP, own_recv)
     for c in range(UNITS):
         whole(far_in, c * LANES, LANES, far_recv.at[c])

time: 45.8 us -> 46.5 us (1.015)
  Pallas kernels: 45 us -> 45.7 us
    pallas_call x1, Pallas kernels: 44 us -> 44.7 us  [per_device(): pl.pallas_call(kernel, out_shape=(grid, grid), in_specs=[hbm] * 7, out_sp...]
where the time goes in v11:
time: 46.5 us; the launch traced here: 46.3 us
  Pallas kernels  45.7 us (98%)
  between operations  0.64 us (1%)
    pallas_call x1, Pallas kernels, per_device(): pl.pallas_call(kernel, out_shape=(grid, grid), in_specs=[hbm] * 7, out_sp...  44.7 us
    pallas_call x1, Pallas kernels, per_device(): pl.pallas_call(store, out_shape=(grid, grid), in_specs=[local, local], ou...  0.99 us

profile of v11, /device:TPU:0, one launch (start us, length us, event | category | flops | bytes accessed | tf_op | source)
XLA Modules:
  0.0 46.3 jit_solution(1865500175922756887)
XLA Ops:
  0.6 44.7 %dual_step.1 = (f32[4,256,128]{2,1,0:T(8,128)S(1)}, f32[4,256,128]{2,1,0:T(8,128)S(1)}) custom-call(f32[4,256,128]{2,1,0:T(8,128)} %source_ref.1, f32[4,256,128]{2,1,0:T(8,128)} %target_ref.1, f32[4,256,128]{2,1,0:T(8,128)} %potential_ref.1, s32[4,128]{1,0:T(4,128)} %bitcast.9, s32[4,128]{1,0:T(4,128)} %bitcast.10, s32[4,128]{1,0:T(4,128)} %bitcast.11, ...), custom_call_target="tpu_custom_call" | custom-call | tf_op jit(solution)/shard_map/dual_step/pallas_call | solution.py:625
  45.3 1.0 %store.1 = (f32[4,256,128]{2,1,0:T(8,128)}, f32[4,256,128]{2,1,0:T(8,128)}) custom-call(f32[4,256,128]{2,1,0:T(8,128)S(1)} %get-tuple-element.4.pushed_ref, f32[4,256,128]{2,1,0:T(8,128)S(1)} %get-tuple-element.5.next_ref), custom_call_target="tpu_custom_call" | custom-call | tf_op jit(solution)/shard_map/store/pallas_call | solution.py:682
